TPU v7x, 256 devices: a whole 4x4x8 slice. The times are simulated.
256 devices in a mesh: dp: 8 (over z), label: 16 (over x, y), section: 2 (over core).
Axes of the slice: x: 4, y: 4, z: 8, core: 2. Of those that a mesh axis runs over, the one named last changes fastest.
Arguments:
- queries: bfloat16 [32768, 1024], P(('dp', 'label', 'section')), may hold values from -6 to 6
- label_weights: bfloat16 [128, 128, 1024], P('label'), may hold values from -0.1875 to 0.1875
- propensity: float32 [128, 128], P('label'), may hold values from 0.1 to 1
- positives: int32 [32768, 8], P(('dp', 'label', 'section')), may hold values from 0 to 6143
- shortlist: int32 [128, 48], P(('dp', 'label')), may hold values from 0 to 127, as said below
- owner_map: int32 [128], replicated, may hold values from 0 to 127, as said below
Outputs:
- query_grad: float32 [32768, 1024], P(('dp', 'label', 'section'))
- weight_grad: float32 [128, 128, 1024], P('label', ('dp', 'section'))
Inputs may be any that keep to these rules, and one draw needn't show every extreme that they name: owner_map is a permutation of the 128 row blocks. `shortlist`: each row lists 48 different label-block ids. Of one row's blocks at most 6 are stored in the row blocks of one owner (rows o * 8 to o * 8 + 7 of label_weights), and in every draw one owner holds exactly 6 of the blocks of every row.
All inputs are finite; a program needn't handle non-finite values.
Results may differ from a plain program's by a relative error of at most 0.0021.
Values may be sent and summed in bfloat16 or wider, within the bound.
A program may use at most 128 MiB of HBM per device.

v0:
```python
import jax
import jax.numpy as jnp
from jax import lax
from jax.sharding import PartitionSpec as P

grad_scale = 0.25


def per_device(queries, label_weights, propensity, positives, shortlist, owner_map):
    label_count = lax.axis_size("label")
    own_index = lax.axis_index("label")
    peer_rows, peer_pos, peer_lists = (
        lax.all_gather(queries, "label", axis=0, tiled=True),
        lax.all_gather(positives, "label", axis=0, tiled=True),
        lax.all_gather(shortlist, "label", axis=0, tiled=True),
    )
    block_count, block_rows, feature_dim = label_weights.shape
    half_rows = queries.shape[0]
    short_len = peer_lists.shape[1]
    capacity = 2 * short_len // label_count
    table_len = owner_map.shape[0]
    lookup = (
        peer_lists[:, :, None] == jnp.arange(table_len, dtype=jnp.int32)[None, None, :]
    ).astype(jnp.int32)
    stored = jnp.sum(lookup * owner_map[None, None, :], axis=2)
    owners = stored // block_count
    local_slot = stored % block_count
    own_entry = (owners == own_index).astype(jnp.int32)
    entry_rank = jnp.cumsum(own_entry, axis=1) - 1
    select = own_entry[:, :, None] * (
        entry_rank[:, :, None] == jnp.arange(capacity, dtype=jnp.int32)[None, None, :]
    ).astype(jnp.int32)
    slot_ids = jnp.sum(select * local_slot[:, :, None], axis=1)
    entries = jnp.sum(select * jnp.arange(short_len, dtype=jnp.int32)[None, :, None], axis=1)
    live_slot = jnp.sum(select, axis=1).astype(jnp.float32)
    tokens = peer_rows.reshape(label_count, half_rows, feature_dim)
    pos_rows = peer_pos.reshape(label_count, half_rows, -1)
    label_offsets = jnp.arange(block_rows, dtype=jnp.int32)

    def slot_grad(slot_index, score_grads):
        slot_col = lax.dynamic_index_in_dim(slot_ids, slot_index, 1, keepdims=False)
        entry_col = lax.dynamic_index_in_dim(entries, slot_index, 1, keepdims=False)
        live_col = lax.dynamic_index_in_dim(live_slot, slot_index, 1, keepdims=False)
        weights_sel = jnp.take(label_weights, slot_col, axis=0)
        prop_sel = jnp.take(propensity, slot_col, axis=0)
        scores = jnp.einsum("jqd,jld->jql", tokens, weights_sel, preferred_element_type=jnp.float32)
        label_ids = entry_col[:, None] * block_rows + label_offsets[None, :]
        target = jnp.any(pos_rows[:, :, :, None] == label_ids[:, None, None, :], axis=2).astype(
            jnp.float32
        )
        gradient = (
            (jax.nn.sigmoid(scores) - target / prop_sel[:, None, :])
            * live_col[:, None, None]
            * grad_scale
        )
        return lax.dynamic_update_index_in_dim(
            score_grads, gradient.astype(jnp.bfloat16), slot_index, 1
        )

    empty_grads = jnp.zeros((label_count, capacity, half_rows, block_rows), jnp.bfloat16)
    score_grads = lax.fori_loop(0, capacity, slot_grad, empty_grads)
    number = lax.axis_size("label") * half_rows // half_rows
    grad_part = score_grads

    def add_slot(slot_index, running):
        slot_col = lax.dynamic_index_in_dim(slot_ids, slot_index, 1, keepdims=False)
        weights_sel = jnp.take(label_weights, slot_col, axis=0)
        grad_col = lax.dynamic_index_in_dim(grad_part, slot_index, 1, keepdims=False)
        return running + jnp.einsum(
            "jql,jld->jqd", grad_col, weights_sel, preferred_element_type=jnp.float32
        )

    running = lax.fori_loop(
        0, capacity, add_slot, jnp.zeros((number, half_rows, feature_dim), jnp.float32)
    )
    query_grad = lax.psum_scatter(
        running.reshape(lax.axis_size("label") * half_rows, feature_dim),
        "label",
        scatter_dimension=0,
        tiled=True,
    )
    onehot = (
        slot_ids[None, :, :] == jnp.arange(block_count, dtype=jnp.int32)[:, None, None]
    ).astype(jnp.bfloat16)
    picked = jnp.einsum(
        "bjk,jkql->bjql", onehot, score_grads, preferred_element_type=jnp.float32
    ).astype(jnp.bfloat16)
    weight_part = jnp.einsum("bjql,jqd->bld", picked, tokens, preferred_element_type=jnp.float32)
    weight_grad = lax.psum_scatter(weight_part, ("dp", "section"), scatter_dimension=1, tiled=True)
    return (query_grad, weight_grad)


def solution(mesh):
    in_specs = (
        P(("dp", "label", "section"), None),
        P("label", None, None),
        P("label", None),
        P(("dp", "label", "section"), None),
        P(("dp", "label"), None),
        P(),
    )
    out_specs = (P(("dp", "label", "section"), None), P("label", ("dp", "section"), None))
    return jax.shard_map(
        per_device, mesh=mesh, in_specs=in_specs, out_specs=out_specs, check_vma=False
    )
```

profile of v0, /device:TPU:32, one launch (start us, length us, event | category | flops | bytes accessed | tf_op | source)
XLA Modules:
  0.0 348.3 jit_solution(954278934343710310)
XLA Ops:
  8.0 21.0 %all-gather = s32[16,1,48]{2,1,0:T(1,128)S(1)} all-gather(s32[1,1,48]{2,1,0:T(1,128)} %bitcast.77), channel_id=1, replica_groups=mesh['dp'=8,'label'=16,'section'=2] {'label'}, dimensions={0}, use_global_device_ids=true | all-gather | bytes 3264 | tf_op jit(solution)/shard_map/all_gather | solution.py:15
  31.6 25.1 %all_gather.11 = s32[2048,8]{1,0:T(8,128)S(1)} all-gather(s32[128,8]{1,0:T(8,128)S(1)} %copy.15), channel_id=1, replica_groups=mesh['dp'=8,'label'=16,'section'=2] {'label'}, dimensions={0}, use_global_device_ids=true | all-gather | bytes 69632 | tf_op jit(solution)/shard_map/all_gather | solution.py:14
  56.6 13.8 %all-gather.3.cloned.1.call-done = bf16[2048,1024]{1,0:T(8,128)(2,1)} async-done(((bf16[128,1024]{1,0:T(8,128)(2,1)}), bf16[2048,1024]{1,0:T(8,128)(2,1)}) %all-gather.3.cloned.1.call-update) | async-done | bytes 4194320 | tf_op jit(solution)/shard_map/all_gather | solution.py:13
  70.4 90.8 %while.28 = (s32[]{:T(128)}, bf16[16,6,128,128]{2,3,0,1:T(8,128)(2,1)}, s32[16,6]{0,1:T(8,128)S(1)}, bf16[8,128,1024]{2,1,0:T(8,128)(2,1)}, bf16[16,128,1024]{2,...) while((s32[]{:T(128)}, ...), condition=%wide.region_7.9_spmd.clone, body=%wide.region_5.8_spmd.clone.sunk | while | flops 545265856 | bytes 18482240 | solution.py:61
  75.5 4.4 %gather_fusion = bf16[16,128,1024]{2,1,0:T(8,128)(2,1)} fusion(bf16[8,128,1024]{2,1,0:T(8,128)(2,1)} %get-tuple-element.481, s32[1024]{0:T(1024)S(1)} %pad_clamp_fusion.6), kind=kCustom, calls=%fused_computation.clone.clone.1 | custom fusion | bytes 8388672 | tf_op jit(solution)/shard_map/while/body/eval_jaxpr/jit(_take)/gather | solution.py:44
  79.8 5.7 %fusion.81 = bf16[16,6,128,128]{2,3,0,1:T(8,128)(2,1)} fusion(bf16[16,6,128,128]{2,3,0,1:T(8,128)(2,1)} %get-tuple-element.469, s32[]{:T(128)S(6)} %copy.32, bf16[16,128,1024]{2,1,0:T(8,128)(2,1)} %get-tuple-element.482, bf16[16,128,1024]{2,1,0:T(8,128)(2,1)} %gather_fusion, pred[16]{0:T(512)(128)(4,1)S(1)} %get-tuple-element.448, ...), kind=kOutput, calls=%fused_computation.19.clone.1 | convolution fusion | flops 541327360 | bytes 9183316 | tf_op jit(solution)/shard_map/while/body/eval_jaxpr/jqd,jld->jql/dot_general | solution.py:46
  90.6 4.4 %gather_fusion = bf16[16,128,1024]{2,1,0:T(8,128)(2,1)} fusion(bf16[8,128,1024]{2,1,0:T(8,128)(2,1)} %get-tuple-element.481, s32[1024]{0:T(1024)S(1)} %pad_clamp_fusion.6), kind=kCustom, calls=%fused_computation.clone.clone.1 | custom fusion | bytes 8388672 | tf_op jit(solution)/shard_map/while/body/eval_jaxpr/jit(_take)/gather | solution.py:44
  95.0 5.7 %fusion.81 = bf16[16,6,128,128]{2,3,0,1:T(8,128)(2,1)} fusion(bf16[16,6,128,128]{2,3,0,1:T(8,128)(2,1)} %get-tuple-element.469, s32[]{:T(128)S(6)} %copy.32, bf16[16,128,1024]{2,1,0:T(8,128)(2,1)} %get-tuple-element.482, bf16[16,128,1024]{2,1,0:T(8,128)(2,1)} %gather_fusion, pred[16]{0:T(512)(128)(4,1)S(1)} %get-tuple-element.448, ...), kind=kOutput, calls=%fused_computation.19.clone.1 | convolution fusion | flops 541327360 | bytes 9183316 | tf_op jit(solution)/shard_map/while/body/eval_jaxpr/jqd,jld->jql/dot_general | solution.py:46
  110.1 5.7 %fusion.81 = bf16[16,6,128,128]{2,3,0,1:T(8,128)(2,1)} fusion(bf16[16,6,128,128]{2,3,0,1:T(8,128)(2,1)} %get-tuple-element.469, s32[]{:T(128)S(6)} %copy.32, bf16[16,128,1024]{2,1,0:T(8,128)(2,1)} %get-tuple-element.482, bf16[16,128,1024]{2,1,0:T(8,128)(2,1)} %gather_fusion, pred[16]{0:T(512)(128)(4,1)S(1)} %get-tuple-element.448, ...), kind=kOutput, calls=%fused_computation.19.clone.1 | convolution fusion | flops 541327360 | bytes 9183316 | tf_op jit(solution)/shard_map/while/body/eval_jaxpr/jqd,jld->jql/dot_general | solution.py:46
  120.9 4.4 %gather_fusion = bf16[16,128,1024]{2,1,0:T(8,128)(2,1)} fusion(bf16[8,128,1024]{2,1,0:T(8,128)(2,1)} %get-tuple-element.481, s32[1024]{0:T(1024)S(1)} %pad_clamp_fusion.6), kind=kCustom, calls=%fused_computation.clone.clone.1 | custom fusion | bytes 8388672 | tf_op jit(solution)/shard_map/while/body/eval_jaxpr/jit(_take)/gather | solution.py:44
  125.3 5.7 %fusion.81 = bf16[16,6,128,128]{2,3,0,1:T(8,128)(2,1)} fusion(bf16[16,6,128,128]{2,3,0,1:T(8,128)(2,1)} %get-tuple-element.469, s32[]{:T(128)S(6)} %copy.32, bf16[16,128,1024]{2,1,0:T(8,128)(2,1)} %get-tuple-element.482, bf16[16,128,1024]{2,1,0:T(8,128)(2,1)} %gather_fusion, pred[16]{0:T(512)(128)(4,1)S(1)} %get-tuple-element.448, ...), kind=kOutput, calls=%fused_computation.19.clone.1 | convolution fusion | flops 541327360 | bytes 9183316 | tf_op jit(solution)/shard_map/while/body/eval_jaxpr/jqd,jld->jql/dot_general | solution.py:46
  136.0 4.4 %gather_fusion = bf16[16,128,1024]{2,1,0:T(8,128)(2,1)} fusion(bf16[8,128,1024]{2,1,0:T(8,128)(2,1)} %get-tuple-element.481, s32[1024]{0:T(1024)S(1)} %pad_clamp_fusion.6), kind=kCustom, calls=%fused_computation.clone.clone.1 | custom fusion | bytes 8388672 | tf_op jit(solution)/shard_map/while/body/eval_jaxpr/jit(_take)/gather | solution.py:44
  140.4 5.7 %fusion.81 = bf16[16,6,128,128]{2,3,0,1:T(8,128)(2,1)} fusion(bf16[16,6,128,128]{2,3,0,1:T(8,128)(2,1)} %get-tuple-element.469, s32[]{:T(128)S(6)} %copy.32, bf16[16,128,1024]{2,1,0:T(8,128)(2,1)} %get-tuple-element.482, bf16[16,128,1024]{2,1,0:T(8,128)(2,1)} %gather_fusion, pred[16]{0:T(512)(128)(4,1)S(1)} %get-tuple-element.448, ...), kind=kOutput, calls=%fused_computation.19.clone.1 | convolution fusion | flops 541327360 | bytes 9183316 | tf_op jit(solution)/shard_map/while/body/eval_jaxpr/jqd,jld->jql/dot_general | solution.py:46
  155.5 5.7 %fusion.81 = bf16[16,6,128,128]{2,3,0,1:T(8,128)(2,1)} fusion(bf16[16,6,128,128]{2,3,0,1:T(8,128)(2,1)} %get-tuple-element.469, s32[]{:T(128)S(6)} %copy.32, bf16[16,128,1024]{2,1,0:T(8,128)(2,1)} %get-tuple-element.482, bf16[16,128,1024]{2,1,0:T(8,128)(2,1)} %gather_fusion, pred[16]{0:T(512)(128)(4,1)S(1)} %get-tuple-element.448, ...), kind=kOutput, calls=%fused_computation.19.clone.1 | convolution fusion | flops 541327360 | bytes 9183316 | tf_op jit(solution)/shard_map/while/body/eval_jaxpr/jqd,jld->jql/dot_general | solution.py:46
  161.2 6.2 %copy.18 = bf16[16,6,128,128]{3,1,2,0:T(8,128)(2,1)} copy(bf16[16,6,128,128]{2,3,0,1:T(8,128)(2,1)} %get-tuple-element.490) | data formatting | bytes 6291456 | tf_op jit(solution)/shard_map/while | solution.py:61
  171.1 6.1 %fusion.55 = f32[8,128,1024]{2,1,0:T(8,128)} fusion(bf16[16,128,1024,1]{2,1,0,3:T(8,128)(2,1)S(1)} %bitcast.79, bf16[8,16,128,128]{3,0,2,1:T(8,128)(2,1)S(1)} %convert_bitcast_fusion), kind=kOutput, calls=%fused_computation.50 | convolution fusion | flops 4294967296 | bytes 12582912 | tf_op jit(solution)/shard_map/bjql,jqd->bld/dot_general | solution.py:88
  178.7 72.2 %while.29 = (s32[]{:T(128)}, f32[16,128,1024]{2,1,0:T(8,128)}, bf16[16,6,128,128]{2,3,0,1:T(8,128)(2,1)}, s32[16,6]{0,1:T(8,128)S(1)}, bf16[8,128,1024]{2,1,0:T(8,128)(2,1)S(1)}, /*index=5*/s32[]{:T(128)}, s32[]{:T(128)}) while((s32[]{:T(128)}, f32[16,128,1024]{2,1,0:T(8,128)}, bf16[16,6,128,128]{2,3,0,1:T(8,128)(2,1)}, ...), condition=%wide.region_9.11_spmd.clone, body=%wide.region_8.10_spmd.clone.sunk | while | flops 543163520 | bytes 29888900 | solution.py:73
  181.5 7.1 %select_add_fusion.2 = f32[16,128,1024]{2,1,0:T(8,128)} fusion(f32[16,128,1024]{2,1,0:T(8,128)} %get-tuple-element.496, pred[]{:T(512)S(6)} %compare.18, bf16[16,128,1024]{2,1,0:T(8,128)(2,1)} %gather_fusion.2, pred[16]{0:T(512)(128)(4,1)S(1)} %get-tuple-element.457, bf16[16,6,128,128]{2,3,0,1:T(8,128)(2,1)} %get-tuple-element.504, s32[]{:T(128)S(6)} %copy.38), kind=kOutput, calls=%fused_computation.35.clone.1 | convolution fusion | flops 543162368 | bytes 21495828 | tf_op jit(solution)/shard_map/while/body/eval_jaxpr/jql,jld->jqd/dot_general | solution.py:69
  191.4 9.7 %select_add_fusion.2 = f32[16,128,1024]{2,1,0:T(8,128)} fusion(f32[16,128,1024]{2,1,0:T(8,128)} %get-tuple-element.496, pred[]{:T(512)S(6)} %compare.18, bf16[16,128,1024]{2,1,0:T(8,128)(2,1)} %gather_fusion.2, pred[16]{0:T(512)(128)(4,1)S(1)} %get-tuple-element.457, bf16[16,6,128,128]{2,3,0,1:T(8,128)(2,1)} %get-tuple-element.504, s32[]{:T(128)S(6)} %copy.38), kind=kOutput, calls=%fused_computation.35.clone.1 | convolution fusion | flops 543162368 | bytes 21495828 | tf_op jit(solution)/shard_map/while/body/eval_jaxpr/jql,jld->jqd/dot_general | solution.py:69
  203.8 9.7 %select_add_fusion.2 = f32[16,128,1024]{2,1,0:T(8,128)} fusion(f32[16,128,1024]{2,1,0:T(8,128)} %get-tuple-element.496, pred[]{:T(512)S(6)} %compare.18, bf16[16,128,1024]{2,1,0:T(8,128)(2,1)} %gather_fusion.2, pred[16]{0:T(512)(128)(4,1)S(1)} %get-tuple-element.457, bf16[16,6,128,128]{2,3,0,1:T(8,128)(2,1)} %get-tuple-element.504, s32[]{:T(128)S(6)} %copy.38), kind=kOutput, calls=%fused_computation.35.clone.1 | convolution fusion | flops 543162368 | bytes 21495828 | tf_op jit(solution)/shard_map/while/body/eval_jaxpr/jql,jld->jqd/dot_general | solution.py:69
  216.3 9.7 %select_add_fusion.2 = f32[16,128,1024]{2,1,0:T(8,128)} fusion(f32[16,128,1024]{2,1,0:T(8,128)} %get-tuple-element.496, pred[]{:T(512)S(6)} %compare.18, bf16[16,128,1024]{2,1,0:T(8,128)(2,1)} %gather_fusion.2, pred[16]{0:T(512)(128)(4,1)S(1)} %get-tuple-element.457, bf16[16,6,128,128]{2,3,0,1:T(8,128)(2,1)} %get-tuple-element.504, s32[]{:T(128)S(6)} %copy.38), kind=kOutput, calls=%fused_computation.35.clone.1 | convolution fusion | flops 543162368 | bytes 21495828 | tf_op jit(solution)/shard_map/while/body/eval_jaxpr/jql,jld->jqd/dot_general | solution.py:69
  228.8 9.7 %select_add_fusion.2 = f32[16,128,1024]{2,1,0:T(8,128)} fusion(f32[16,128,1024]{2,1,0:T(8,128)} %get-tuple-element.496, pred[]{:T(512)S(6)} %compare.18, bf16[16,128,1024]{2,1,0:T(8,128)(2,1)} %gather_fusion.2, pred[16]{0:T(512)(128)(4,1)S(1)} %get-tuple-element.457, bf16[16,6,128,128]{2,3,0,1:T(8,128)(2,1)} %get-tuple-element.504, s32[]{:T(128)S(6)} %copy.38), kind=kOutput, calls=%fused_computation.35.clone.1 | convolution fusion | flops 543162368 | bytes 21495828 | tf_op jit(solution)/shard_map/while/body/eval_jaxpr/jql,jld->jqd/dot_general | solution.py:69
  241.3 9.5 %select_add_fusion.2 = f32[16,128,1024]{2,1,0:T(8,128)} fusion(f32[16,128,1024]{2,1,0:T(8,128)} %get-tuple-element.496, pred[]{:T(512)S(6)} %compare.18, bf16[16,128,1024]{2,1,0:T(8,128)(2,1)} %gather_fusion.2, pred[16]{0:T(512)(128)(4,1)S(1)} %get-tuple-element.457, bf16[16,6,128,128]{2,3,0,1:T(8,128)(2,1)} %get-tuple-element.504, s32[]{:T(128)S(6)} %copy.38), kind=kOutput, calls=%fused_computation.35.clone.1 | convolution fusion | flops 543162368 | bytes 21495828 | tf_op jit(solution)/shard_map/while/body/eval_jaxpr/jql,jld->jqd/dot_general | solution.py:69
  250.9 90.8 %reduce-scatter.3.cloned.1.call-done = f32[128,1024]{1,0:T(8,128)} async-done(((f32[2048,1024]{1,0:T(8,128)}), f32[128,1024]{1,0:T(8,128)}) %reduce-scatter.3.cloned.1.call-update) | async-done | bytes 524304 | tf_op jit(solution)/shard_map/reduce_scatter | solution.py:76
  (108 shorter events, 64.2 us)
Async XLA Ops:
  7.2 63.2 %all-gather.3.cloned.1.call-start = ((), (), s32[]{:S(2)}) async-start(), calls=%async_computation.2 | async-start | bytes 4456448 | tf_op jit(solution)/shard_map/all_gather | solution.py:13
  7.9 243.0 %reduce-scatter.5.cloned.1.call-start = ((), (), s32[]{:S(2)}) async-start(), calls=%async_computation.4 | async-start | bytes 4456448 | tf_op jit(solution)/shard_map/reduce_scatter | solution.py:89
  167.5 3.6 %copy-start.1 = (bf16[16,128,1024]{2,1,0:T(8,128)(2,1)S(1)}, bf16[16,128,1024]{2,1,0:T(8,128)(2,1)}, u32[]{:S(2)}) copy-start(bf16[16,128,1024]{2,1,0:T(8,128)(2,1)} %get-tuple-element.521) | copy-start | bytes 12582916
  177.1 1.6 copy-start
  177.1 164.6 %reduce-scatter.3.cloned.1.call-start = ((), (), s32[]{:S(2)}) async-start(), calls=%async_computation.3 | async-start | bytes 8912896 | tf_op jit(solution)/shard_map/reduce_scatter | solution.py:76
Sparse Core Ops, SparseCore 0:
  10.4 59.9 all-gather.2
  177.3 59.6 reduce-scatter.4
  251.0 90.6 reduce-scatter.2
where the time goes:
time: 349 us; the launch traced here: 348 us
  waiting for transfers between devices  105 us (30%)
  matrix products  99.1 us (28%)
  local copies, waits for them, and re-layouts  61.1 us (18%)
  blocking collectives  46 us (13%)
  other arithmetic  22.4 us (6%)
  between operations  13.8 us (4%)
    reduce_scatter x1, waiting for transfers between devices, per_device(): lax.psum_scatter(running.reshape(lax.axis_size('label') * half_rows, feat...  90.8 us
    dot_general x6, matrix products, add_slot(): jnp.einsum('jql,jld->jqd', grad_col, weights_sel, preferred_element_type=...  55.4 us
    dot_general x6, matrix products, slot_grad(): jnp.einsum('jqd,jld->jql', tokens, weights_sel, preferred_element_type=jn...  34.1 us
    gather x6, local copies, waits for them, and re-layouts, slot_grad(): weights_sel = jnp.take(label_weights, slot_col, axis=0)  26.3 us
    all_gather x1, blocking collectives, per_device(): lax.all_gather(positives, 'label', axis=0, tiled=True)  25.1 us
    all_gather x1, blocking collectives, per_device(): lax.all_gather(shortlist, 'label', axis=0, tiled=True)  21 us
    reduce_or x6, other arithmetic, slot_grad(): jnp.any(pos_rows[:, :, :, None] == label_ids[:, None, None, :], axis=2)  19.4 us
    gather x6, local copies, waits for them, and re-layouts, add_slot(): weights_sel = jnp.take(label_weights, slot_col, axis=0)  16.6 us
  transfers between devices with their start and end apart: 3, of which 2 were waited for; matrix products, arithmetic and copies ran while one was open for 21% of the time, Pallas kernels for 0%

commit v1 on v0

v1 whole, which is shorter than its diff:
```python
import functools

import jax
import jax.numpy as jnp
from jax import lax
from jax.experimental import pallas as pl
from jax.experimental.pallas import tpu as pltpu
from jax.sharding import PartitionSpec as P

MESH = pl.DeviceIdType.MESH
SIDE = 4
RING = 8
HALF = 64
QUART = 32
grad_scale = 0.25
F32, BF16 = jnp.float32, jnp.bfloat16


def kernel(
    q_ref, w_ref, invp_ref, meta_ref, qg_ref, wo_ref,
    q_all, part, wg, sg, meta_all, pos_t, labid,
    s1s, s1r, s2r, xr, zr,
    ag_ss, ag_rs, me_ss, me_rs, s1_ss, s1_rs, s2_ss, s2_rs, x_ss, x_rs, z_ss, z_rs, loc_s,
):
    label = lax.axis_index("label")
    z = lax.axis_index("dp")
    core = lax.axis_index("section")
    x, y = label // SIDE, label % SIDE

    def at(dx, dy):
        return {"label": lax.rem(x + dx + SIDE, SIDE) * SIDE + lax.rem(y + dy + SIDE, SIDE)}

    def along(axis, d):
        return at(d, 0) if axis == 0 else at(0, d)

    def slow(c, d):
        return along(c, d)

    def fast(c, d):
        return along(1 - c, d)

    def zdev(d):
        return {"dp": lax.rem(z + d + RING, RING)}

    other = {"section": 1 - core}

    peers = [at(d, 0) for d in (1, 2, 3)] + [at(0, d) for d in (1, 2, 3)] + [zdev(1), zdev(-1), other]
    barrier = pltpu.get_barrier_semaphore()
    for peer in peers:
        pl.semaphore_signal(barrier, inc=1, device_id=peer, device_id_type=MESH)
    pl.semaphore_wait(barrier, len(peers))

    def remote(src, dst, ss, rs, dev):
        return pltpu.make_async_remote_copy(
            src_ref=src, dst_ref=dst, send_sem=ss, recv_sem=rs, device_id=dev, device_id_type=MESH
        )

    started = []

    def go(copy):
        copy.start()
        started.append(copy)
        return copy

    lo, hi = pl.ds(0, QUART), pl.ds(QUART, QUART)
    ag = {}

    def ag_send(c, slot, kind, src, dst, dev):
        ag[c, slot, kind] = go(remote(src, dst, ag_ss.at[c, slot, kind], ag_rs.at[c, slot, kind], dev))

    def p1a(c):
        ag_send(c, 4, 0, q_ref.at[c], q_all.at[0, c, 3], slow(c, 1))
        ag_send(c, 4, 1, q_ref.at[c], q_all.at[0, c, 1], slow(c, -1))

    def p1b(c, kind):
        ag[c, 4, kind].wait_recv()
        if kind == 0:
            ag_send(c, 4, 2, q_all.at[0, c, 3, lo], q_all.at[0, c, 2, lo], slow(c, 1))
        else:
            ag_send(c, 4, 3, q_all.at[0, c, 1, hi], q_all.at[0, c, 2, hi], slow(c, -1))

    def p2a(c, j):
        src = q_ref.at[c] if j == 0 else q_all.at[0, c, j]
        ag_send(c, j, 0, src, q_all.at[3, c, j], fast(c, 1))
        ag_send(c, j, 1, src, q_all.at[1, c, j], fast(c, -1))

    def p2b(c, j):
        ag[c, j, 0].wait_recv()
        ag_send(c, j, 2, q_all.at[3, c, j, lo], q_all.at[2, c, j, lo], fast(c, 1))
        ag[c, j, 1].wait_recv()
        ag_send(c, j, 3, q_all.at[1, c, j, hi], q_all.at[2, c, j, hi], fast(c, -1))

    p1a(0)
    p1a(1)
    locals_ = [
        pltpu.make_async_copy(meta_ref, meta_all.at[0, 0], loc_s.at[0]),
        pltpu.make_async_copy(q_ref.at[0], q_all.at[0, 0, 0], loc_s.at[1]),
        pltpu.make_async_copy(q_ref.at[1], q_all.at[0, 1, 0], loc_s.at[2]),
    ]
    for copy in locals_:
        copy.start()
    meta_x = [
        go(remote(meta_ref, meta_all.at[SIDE - a, 0], me_ss.at[0, a], me_rs.at[0, a], at(a, 0)))
        for a in (1, 2, 3)
    ]
    p2a(0, 0)
    p2a(1, 0)
    for copy in locals_:
        copy.wait()
    wg[...] = jnp.zeros_like(wg)
    for copy in meta_x:
        copy.wait_recv()
    meta_y = [
        go(remote(meta_all.at[:, 0], meta_all.at[:, SIDE - a], me_ss.at[1, a], me_rs.at[1, a], at(0, a)))
        for a in (1, 2, 3)
    ]
    for c in (0, 1):
        p1b(c, 0)
        p1b(c, 1)
    for c in (0, 1):
        p2a(c, 3)
        p2a(c, 1)
    for copy in meta_y:
        copy.wait_recv()

    def prepare(d, carry):
        dx, dy = d // SIDE, d % SIDE
        tile = meta_all[dx, dy]
        pos_t[d] = jnp.transpose(tile[0:8, :])
        lane = lax.broadcasted_iota(jnp.int32, (8, 128), 1)
        sub = lax.broadcasted_iota(jnp.int32, (8, 128), 0)
        entry = jnp.sum(
            jnp.where(lane == label * 8 + sub, jnp.broadcast_to(tile[8:9, :], (8, 128)), 0),
            axis=1, keepdims=True,
        )
        labid[d] = jnp.where(entry >= 0, entry * 128 + lane, -1)
        return carry

    lax.fori_loop(0, SIDE * SIDE, prepare, 0)
    for c in (0, 1):
        ag[c, 4, 2].wait_recv()
        ag[c, 4, 3].wait_recv()
        p2a(c, 2)
    for c in (0, 1):
        p2b(c, 0)

    def score_chunk(k):
        def body(n, carry):
            rows = q_all[k].reshape(2 * SIDE * HALF, 1024)
            s = lax.dot_general(
                rows, w_ref[pl.ds(pl.multiple_of(n * 256, 256), 256), :],
                (((1,), (1,)), ((), ())), preferred_element_type=F32,
            )
            for c in (0, 1):
                for j in range(SIDE):
                    dev = j * SIDE + k if c == 0 else k * SIDE + j
                    r0 = (c * SIDE + j) * HALF
                    pos = pos_t[dev, c * HALF : (c + 1) * HALF, :]
                    cols = [jnp.broadcast_to(pos[:, p : p + 1], (HALF, 128)) for p in range(8)]
                    for b in (0, 1):
                        ids = labid[dev, pl.ds(2 * n + b, 1), :]
                        inv = invp_ref[pl.ds(2 * n + b, 1), :]
                        hit = cols[0] == ids
                        for p in range(1, 8):
                            hit = hit | (cols[p] == ids)
                        sig = jax.nn.sigmoid(s[r0 : r0 + HALF, b * 128 : (b + 1) * 128])
                        g = (sig - jnp.where(hit, inv, 0.0)) * jnp.where(ids >= 0, grad_scale, 0.0)
                        sg[r0 : r0 + HALF, pl.ds(pl.multiple_of(n * 256 + b * 128, 128), 128)] = g.astype(BF16)
            return carry

        lax.fori_loop(0, 4, body, 0)

    def query_chunk(k):
        def body(n, carry):
            cols = pl.ds(pl.multiple_of(n * 256, 256), 256)
            part[k, :, :, :, cols] = jnp.dot(
                sg[...], w_ref[:, cols], preferred_element_type=F32
            ).reshape(2, SIDE, HALF, 256)
            return carry

        lax.fori_loop(0, 4, body, 0)

    def weight_chunk(k):
        def body(n, carry):
            cols = pl.ds(pl.multiple_of(n * 256, 256), 256)
            out = lax.dot_general(
                sg[:, cols], q_all[k].reshape(2 * SIDE * HALF, 1024),
                (((0,), (0,)), ((), ())), preferred_element_type=F32,
            )
            rows = pl.ds(n * 2, 2)
            wg[rows] = wg[rows] + out.reshape(2, 16, 8, 1024)
            return carry

        lax.fori_loop(0, 4, body, 0)

    s1 = {}

    def s1_send(c, d, m, k, half):
        def body(j, carry):
            s1s[c, d, m, j] = part[k, c, j, half * QUART : (half + 1) * QUART, :].astype(BF16)
            return carry

        lax.fori_loop(0, SIDE, body, 0)
        s1[c, d, m] = go(
            remote(s1s.at[c, d, m], s1r.at[c, d, m], s1_ss.at[c, d, m], s1_rs.at[c, d, m], fast(c, 1 - 2 * d))
        )

    def s1_add(c, d, m, k, half):
        s1[c, d, m].wait_recv()

        def body(j, carry):
            rows = slice(half * QUART, (half + 1) * QUART)
            part[k, c, j, rows, :] = part[k, c, j, rows, :] + s1r[c, d, m, j].astype(F32)
            return carry

        lax.fori_loop(0, SIDE, body, 0)

    score_chunk(0)
    for c in (0, 1):
        p2b(c, 3)
    query_chunk(0)
    for c in (0, 1):
        p2b(c, 1)
    weight_chunk(0)
    for c in (0, 1):
        p2b(c, 2)
    score_chunk(3)
    query_chunk(3)
    for c in (0, 1):
        s1_send(c, 1, 1, 3, 0)
    weight_chunk(3)
    score_chunk(1)
    query_chunk(1)
    for c in (0, 1):
        s1_send(c, 0, 1, 1, 1)
    weight_chunk(1)
    for c in (0, 1):
        for j in range(SIDE):
            ag[c, j, 2].wait_recv()
            ag[c, j, 3].wait_recv()
    score_chunk(2)
    query_chunk(2)
    for c in (0, 1):
        s1_send(c, 0, 0, 2, 0)
        s1_send(c, 1, 0, 2, 1)
    weight_chunk(2)

    def piece(r, own):
        return lax.rem(z + r, RING) * 2 + (core if own else 1 - core)

    order = (4, 3, 5, 2, 6, 1, 7, 0)
    ex = {
        r: go(remote(wg.at[:, piece(r, False)], xr.at[r], x_ss.at[r], x_rs.at[r], other)) for r in order
    }

    def ex_add(r):
        ex[r].wait_recv()
        i = piece(r, True)
        wg[:, i] = wg[:, i] + xr[r]

    zc = {}

    def z_send(d, t, h):
        r = 4 - t if d == 0 else 4 + t
        zc[d, t, h] = go(
            remote(
                wg.at[pl.ds(4 * h, 4), piece(r, True)], zr.at[d, t, h],
                z_ss.at[d, t, h], z_rs.at[d, t, h], zdev(1 - 2 * d),
            )
        )

    def z_add(d, t, h):
        zc[d, t, h].wait_recv()
        r = 3 - t if d == 0 else (5 + t) % RING
        i = piece(r, True)
        rows = slice(4 * h, 4 * h + 4)
        wg[rows, i] = wg[rows, i] + zr[d, t, h]

    s2 = {}

    def s2_send(c, d, m, j, half):
        s2[c, d, m] = go(
            remote(
                part.at[0, c, j, pl.ds(half * QUART, QUART)], s2r.at[c, d, m],
                s2_ss.at[c, d, m], s2_rs.at[c, d, m], slow(c, 1 - 2 * d),
            )
        )

    def s2_add(c, d, m, j, half):
        s2[c, d, m].wait_recv()
        rows = slice(half * QUART, (half + 1) * QUART)
        part[0, c, j, rows, :] = part[0, c, j, rows, :] + s2r[c, d, m]

    for c in (0, 1):
        s1_add(c, 1, 1, 0, 0)
        s1_add(c, 0, 1, 0, 1)
    for c in (0, 1):
        s1_add(c, 0, 0, 1, 0)
        s1_send(c, 0, 2, 1, 0)
        s1_add(c, 1, 0, 3, 1)
        s1_send(c, 1, 2, 3, 1)
    for r in (4, 3, 5):
        ex_add(r)
    z_send(0, 0, 0)
    z_send(1, 0, 1)
    z_send(0, 1, 1)
    z_send(1, 1, 0)
    for r in (2, 6, 1, 7, 0):
        ex_add(r)
    z_add(0, 0, 0)
    z_send(0, 1, 0)
    z_add(1, 0, 1)
    z_send(1, 1, 1)
    for c in (0, 1):
        s1_add(c, 0, 2, 0, 0)
        s1_add(c, 1, 2, 0, 1)
        s2_send(c, 0, 0, 2, 0)
        s2_send(c, 1, 0, 2, 1)
        s2_send(c, 0, 1, 1, 1)
        s2_send(c, 1, 1, 3, 0)
    for d, h in ((0, 1), (1, 0), (0, 0), (1, 1)):
        z_add(d, 1, h)
        z_send(d, 2, h)
    for c in (0, 1):
        s2_add(c, 0, 0, 1, 0)
        s2_send(c, 0, 2, 1, 0)
        s2_add(c, 1, 0, 3, 1)
        s2_send(c, 1, 2, 3, 1)
    for d, h in ((0, 1), (1, 0), (0, 0), (1, 1)):
        z_add(d, 2, h)
        z_send(d, 3, h)
    for c in (0, 1):
        s2_add(c, 0, 1, 0, 1)
        s2_add(c, 1, 1, 0, 0)
    for c in (0, 1):
        s2_add(c, 0, 2, 0, 0)
        s2_add(c, 1, 2, 0, 1)
        qg_ref[c] = part[0, c, 0]
    for d, h in ((0, 1), (1, 0), (0, 0), (1, 1)):
        z_add(d, 3, h)
    wo_ref[...] = wg[:, piece(0, True)]
    for copy in started:
        copy.wait_send()


def per_device(queries, label_weights, propensity, positives, shortlist, owner_map):
    blocks, block_rows, dim = label_weights.shape
    table = owner_map.shape[0]
    entries = jnp.arange(shortlist.shape[1], dtype=jnp.int32)
    ids = jnp.arange(table, dtype=jnp.int32)
    lookup = shortlist[0][:, None] == ids[None, :]
    stored = jnp.sum(jnp.where(lookup, owner_map[None, :], 0), axis=1)
    entry_of = jnp.sum(jnp.where(stored[:, None] == ids[None, :], entries[:, None] + 1, 0), axis=0) - 1
    meta = jnp.concatenate(
        [positives.T, entry_of[None, :], jnp.zeros((7, table), jnp.int32)], axis=0
    )
    vm = pl.BlockSpec(memory_space=pltpu.VMEM)
    dma = pltpu.SemaphoreType.DMA
    qg, wo = pl.pallas_call(
        kernel,
        out_shape=(
            jax.ShapeDtypeStruct((2, HALF, dim), F32),
            jax.ShapeDtypeStruct((blocks, 8, dim), F32),
        ),
        in_specs=[vm] * 4,
        out_specs=(vm, vm),
        scratch_shapes=[
            pltpu.VMEM((SIDE, 2, SIDE, HALF, dim), BF16),
            pltpu.VMEM((SIDE, 2, SIDE, HALF, dim), F32),
            pltpu.VMEM((blocks, 16, 8, dim), F32),
            pltpu.VMEM((2 * SIDE * HALF, blocks * block_rows), BF16),
            pltpu.VMEM((SIDE, SIDE, 16, 128), jnp.int32),
            pltpu.VMEM((SIDE * SIDE, 128, 8), jnp.int32),
            pltpu.VMEM((SIDE * SIDE, 8, 128), jnp.int32),
            pltpu.VMEM((2, 2, 3, SIDE, QUART, dim), BF16),
            pltpu.VMEM((2, 2, 3, SIDE, QUART, dim), BF16),
            pltpu.VMEM((2, 2, 3, QUART, dim), F32),
            pltpu.VMEM((RING, blocks, 8, dim), F32),
            pltpu.VMEM((2, 4, 2, 4, 8, dim), F32),
            dma((2, 5, 4)), dma((2, 5, 4)),
            dma((2, 4)), dma((2, 4)),
            dma((2, 2, 3)), dma((2, 2, 3)),
            dma((2, 2, 3)), dma((2, 2, 3)),
            dma((RING,)), dma((RING,)),
            dma((2, 4, 2)), dma((2, 4, 2)),
            dma((3,)),
        ],
        compiler_params=pltpu.CompilerParams(
            collective_id=0, has_side_effects=True, vmem_limit_bytes=60 * 1024 * 1024
        ),
    )(
        queries.reshape(2, HALF, dim),
        label_weights.reshape(blocks * block_rows, dim),
        1.0 / propensity,
        meta,
    )
    return qg.reshape(2 * HALF, dim), wo


def solution(mesh):
    in_specs = (
        P(("dp", "label", "section"), None),
        P("label", None, None),
        P("label", None),
        P(("dp", "label", "section"), None),
        P(("dp", "label"), None),
        P(),
    )
    out_specs = (P(("dp", "label", "section"), None), P("label", ("dp", "section"), None))
    return jax.shard_map(
        per_device, mesh=mesh, in_specs=in_specs, out_specs=out_specs, check_vma=False
    )
```

time: 349 us -> 89.7 us (0.26)
  waiting for transfers between devices: 105 us -> 0 us
  matrix products: 99.1 us -> 0 us
  Pallas kernels: 0 us -> 81.3 us
  local copies, waits for them, and re-layouts: 61.1 us -> 3.63 us
  blocking collectives: 46 us -> 0 us
  other arithmetic: 22.4 us -> 3.6 us
  between operations: 13.8 us -> 0.66 us
    dot_general x14 -> x0, matrix products: 99.1 us -> none  [the longest x6 55.4 us: add_slot(): jnp.einsum('jql,jld->jqd', grad_col, weights_sel, preferred_element_type=...]
    reduce_scatter x2 -> x0, waiting for transfers between devices: 90.9 us -> none  [the longest x1 90.8 us: per_device(): lax.psum_scatter(running.reshape(lax.axis_size('label') * half_rows, feat...]
    pallas_call x0 -> x1, Pallas kernels: none -> 81.3 us  [per_device(): pl.pallas_call(kernel, out_shape=(jax.ShapeDtypeStruct((2, HALF, dim), F3...]
    gather x18 -> x0, local copies, waits for them, and re-layouts: 50.4 us -> none  [the longest x6 26.3 us: slot_grad(): weights_sel = jnp.take(label_weights, slot_col, axis=0)]
    all_gather x2 -> x0, blocking collectives: 46 us -> none  [the longest x1 25.1 us: per_device(): lax.all_gather(positives, 'label', axis=0, tiled=True)]
    reduce_or x6 -> x0, other arithmetic: 19.4 us -> none  [slot_grad(): jnp.any(pos_rows[:, :, :, None] == label_ids[:, None, None, :], axis=2)]
    all_gather x1 -> x0, waiting for transfers between devices: 13.8 us -> none  [per_device(): lax.all_gather(queries, 'label', axis=0, tiled=True)]
    while x1 -> x0, local copies, waits for them, and re-layouts: 6.25 us -> none  [per_device(): score_grads = lax.fori_loop(0, capacity, slot_grad, empty_grads)]
  transfers between devices with their start and end apart: 3 -> 0, of which waited for: 2 -> 0; matrix products, arithmetic and copies ran while one was open for 21% -> 0% of each run, Pallas kernels for 0% -> 0%
where the time goes in v1:
time: 89.7 us; the launch traced here: 89.1 us
  Pallas kernels  81.3 us (91%)
  local copies, waits for them, and re-layouts  3.63 us (4%)
  other arithmetic  3.6 us (4%)
    pallas_call x1, Pallas kernels, per_device(): pl.pallas_call(kernel, out_shape=(jax.ShapeDtypeStruct((2, HALF, dim), F3...  81.3 us
    unnamed x2, local copies, waits for them, and re-layouts  3.56 us

profile of v1, /device:TPU:32, one launch (start us, length us, event | category | flops | bytes accessed | tf_op | source)
XLA Modules:
  0.0 89.1 jit_solution(2873460988343384477)
XLA Ops:
  0.6 0.8 select_reduce_fusion.1
  1.5 0.1 pad.2.clone
  1.6 0.1 select_reduce_fusion
  1.7 1.3 %broadcast_divide_fusion.invp_ref = f32[8,128]{1,0:T(8,128)} fusion(f32[8,128]{1,0:T(8,128)} %param.8), kind=kLoop, calls=%fused_computation.5 | loop fusion | flops 1024 | bytes 8192 | tf_op jit(solution)/shard_map/div | solution.py:394
  3.0 1.4 %add_add_fusion.meta_ref = s32[16,128]{1,0:T(8,128)} fusion(s32[1,128]{1,0:T(1,128)S(1)} %add_bitcast_fusion, s32[8,128]{1,0:T(8,128)} %bitcast.10, s32[16]{0:T(128)S(1)} %pad.2.clone), kind=kLoop, calls=%fused_computation.4 | loop fusion | flops 4096 | bytes 12864 | tf_op jit(solution)/shard_map/concatenate | solution.py:354
  4.3 81.3 %shard_map.77 = (f32[2,64,1024]{2,1,0:T(8,128)}, f32[8,8,1024]{2,1,0:T(8,128)}) custom-call(bf16[2,64,1024]{2,1,0:T(8,128)(2,1)} %bitcast.9, bf16[1024,1024]{1,0:T(8,128)(2,1)} %bitcast.7, f32[8,128]{1,0:T(8,128)} %broadcast_divide_fusion.invp_ref, s32[16,128]{1,0:T(8,128)} %add_add_fusion.meta_ref), custom_call_target="tpu_custom_call" | custom-call | tf_op jit(solution)/shard_map/pallas_call | solution.py:359
  85.6 1.9 %copy.10 = f32[128,1024]{1,0:T(8,128)} copy(f32[128,1024]{1,0:T(8,128)} %bitcast.8) | data formatting | bytes 1048576
  87.5 1.7 %copy.11 = f32[8,8,1024]{2,1,0:T(8,128)} copy(f32[8,8,1024]{2,1,0:T(8,128)} %get-tuple-element.9) | data formatting | bytes 524288
  (3 shorter events, 0.0 us)

commit v2 on v1

v2 whole, which is shorter than its diff:
```python
import jax
import jax.numpy as jnp
from jax import lax
from jax.experimental import pallas as pl
from jax.experimental.pallas import tpu as pltpu
from jax.sharding import PartitionSpec as P

MESH = pl.DeviceIdType.MESH
SIDE = 4
RING = 8
HALF = 64
QUART = 32
TILES = 4
WIDE = 256
FAR = 1 << 20
grad_scale = 0.25
F32, BF16, I32 = jnp.float32, jnp.bfloat16, jnp.int32


def kernel(
    q_hbm, w_hbm, prop_hbm, pos_hbm, list_hbm, map_hbm, qg_ref, wo_ref,
    q_all, w_ref, prop_ref, list_ref, map_ref, meta, meta_all, words_t, live, inv,
    sg, p0, p1, p3, wg, s1s, s1r, s2s, s2r, s3s, s3r, xr, zs, zr, zfs, zfr,
    loc_s, me_ss, me_rs, ag_ss, ag_rs, s1_ss, s1_rs, s2_ss, s2_rs, x_ss, x_rs, z_ss, z_rs,
):
    label = lax.axis_index("label")
    z = lax.axis_index("dp")
    core = lax.axis_index("section")
    x, y = label // SIDE, label % SIDE
    rows_all = 2 * SIDE * HALF
    dim = SIDE * WIDE

    def at(dx, dy):
        return {"label": lax.rem(x + dx + SIDE, SIDE) * SIDE + lax.rem(y + dy + SIDE, SIDE)}

    def along(axis, d):
        return at(d, 0) if axis == 0 else at(0, d)

    def slow(c, d):
        return along(c, d)

    def fast(c, d):
        return along(1 - c, d)

    def zdev(d):
        return {"dp": lax.rem(z + d + RING, RING)}

    other = {"section": 1 - core}

    peers = [at(d, 0) for d in (1, 2, 3)] + [at(0, d) for d in (1, 2, 3)] + [zdev(1), zdev(-1), other]
    barrier = pltpu.get_barrier_semaphore()
    for peer in peers:
        pl.semaphore_signal(barrier, inc=1, device_id=peer, device_id_type=MESH)

    def local(i, src, dst):
        copy = pltpu.make_async_copy(src, dst, loc_s.at[i])
        copy.start()
        return copy

    loc_q = [local(c, q_hbm.at[c], q_all.at[0, c, 0]) for c in (0, 1)]
    loc_m = [local(2, list_hbm, list_ref), local(3, map_hbm, map_ref), local(4, pos_hbm, meta.at[pl.ds(0, 8)])]
    loc_w = [local(5, w_hbm, w_ref), local(6, prop_hbm, prop_ref)]

    for copy in loc_m:
        copy.wait()
    short = list_ref.shape[1]
    sub = lax.broadcasted_iota(I32, (short, short), 0)
    lane = lax.broadcasted_iota(I32, (short, short), 1)
    list_col = jnp.sum(jnp.where(sub == lane, list_ref[...], 0), axis=1, keepdims=True)
    sub = lax.broadcasted_iota(I32, (short, 128), 0)
    lane = lax.broadcasted_iota(I32, (short, 128), 1)
    stored = jnp.sum(jnp.where(list_col == lane, map_ref[...], 0), axis=1, keepdims=True)
    meta[pl.ds(8, 8), :] = jnp.broadcast_to(
        jnp.sum(jnp.where(stored == lane, sub + 1, 0), axis=0, keepdims=True) - 1, (8, 128)
    )
    meta_all[0, 0] = meta[...]

    pl.semaphore_wait(barrier, len(peers))

    def remote(src, dst, ss, rs, dev):
        return pltpu.make_async_remote_copy(
            src_ref=src, dst_ref=dst, send_sem=ss, recv_sem=rs, device_id=dev, device_id_type=MESH
        )

    started = []

    def go(copy):
        copy.start()
        started.append(copy)
        return copy

    lo, hi = pl.ds(0, QUART), pl.ds(QUART, QUART)
    ag = {}

    def ag_send(c, slot, kind, src, dst, dev):
        ag[c, slot, kind] = go(remote(src, dst, ag_ss.at[c, slot, kind], ag_rs.at[c, slot, kind], dev))

    def p1a(c):
        ag_send(c, 4, 0, q_all.at[0, c, 0], q_all.at[0, c, 3], slow(c, 1))
        ag_send(c, 4, 1, q_all.at[0, c, 0], q_all.at[0, c, 1], slow(c, -1))

    def p1b(c, kind):
        ag[c, 4, kind].wait_recv()
        if kind == 0:
            ag_send(c, 4, 2, q_all.at[0, c, 3, lo], q_all.at[0, c, 2, lo], slow(c, 1))
        else:
            ag_send(c, 4, 3, q_all.at[0, c, 1, hi], q_all.at[0, c, 2, hi], slow(c, -1))

    def p2a(c, j):
        ag_send(c, j, 0, q_all.at[0, c, j], q_all.at[3, c, j], fast(c, 1))
        ag_send(c, j, 1, q_all.at[0, c, j], q_all.at[1, c, j], fast(c, -1))

    def p2b(c, j):
        ag[c, j, 0].wait_recv()
        ag_send(c, j, 2, q_all.at[3, c, j, lo], q_all.at[2, c, j, lo], fast(c, 1))
        ag[c, j, 1].wait_recv()
        ag_send(c, j, 3, q_all.at[1, c, j, hi], q_all.at[2, c, j, hi], fast(c, -1))

    for copy in loc_q:
        copy.wait()
    p1a(0)
    p1a(1)
    meta_x = [
        go(remote(meta, meta_all.at[SIDE - a, 0], me_ss.at[0, a], me_rs.at[0, a], at(a, 0)))
        for a in (1, 2, 3)
    ]
    p2a(0, 0)
    p2a(1, 0)
    for copy in meta_x:
        copy.wait_recv()
    meta_y = [
        go(remote(meta_all.at[:, 0], meta_all.at[:, SIDE - a], me_ss.at[1, a], me_rs.at[1, a], at(0, a)))
        for a in (1, 2, 3)
    ]
    for copy in loc_w:
        copy.wait()
    inv[...] = grad_scale / prop_ref[...]
    words_t[...] = jnp.zeros_like(words_t)
    for c in (0, 1):
        p1b(c, 0)
        p1b(c, 1)
    for c in (0, 1):
        p2a(c, 3)
        p2a(c, 1)
    for copy in meta_y:
        copy.wait_recv()

    def prepare(d, carry):
        tile = meta_all[d // SIDE, d % SIDE]
        sub = lax.broadcasted_iota(I32, (QUART, 128), 0)
        lane = lax.broadcasted_iota(I32, (QUART, 128), 1)
        row = tile[8:9, :]
        entry = jnp.sum(jnp.where(lane == label * 8 + sub // 4, row, 0), axis=1, keepdims=True)
        base = jnp.where(entry >= 0, entry * 128 + (sub % 4) * 32, FAR)
        words = jnp.zeros((QUART, 128), I32)
        for p in range(8):
            rel = tile[p : p + 1, :] - base
            words = words | jnp.where((rel >= 0) & (rel < 32), jnp.left_shift(1, rel & 31), 0)
        words_t[d, :, 0:QUART] = jnp.transpose(words)
        sub8 = lax.broadcasted_iota(I32, (8, 128), 0)
        lane8 = lax.broadcasted_iota(I32, (8, 128), 1)
        entry8 = jnp.sum(jnp.where(lane8 == label * 8 + sub8, row, 0), axis=1, keepdims=True)
        live[d] = jnp.broadcast_to(jnp.where(entry8 >= 0, 0.5 * grad_scale, 0.0), (8, 128))
        return carry

    lax.fori_loop(0, SIDE * SIDE, prepare, 0)
    for c in (0, 1):
        ag[c, 4, 2].wait_recv()
        ag[c, 4, 3].wait_recv()
        p2a(c, 2)

    def tile_of(n):
        return pl.ds(pl.multiple_of(n * WIDE, WIDE), WIDE)

    def loop(body):
        def step(n, carry):
            body(n)
            return carry

        lax.fori_loop(0, TILES, step, 0)

    def score_chunk(k):
        def body(n):
            s = lax.dot_general(
                q_all[k].reshape(rows_all, dim), w_ref[tile_of(n), :],
                (((1,), (1,)), ((), ())), preferred_element_type=F32,
            )
            lane = lax.broadcasted_iota(I32, (HALF, 128), 1)
            up = 31 - (lane & 31)
            for c in (0, 1):
                for j in range(SIDE):
                    dev = j * SIDE + k if c == 0 else k * SIDE + j
                    r0 = (c * SIDE + j) * HALF
                    words = words_t[dev, c * HALF : (c + 1) * HALF, :]
                    for b in (0, 1):
                        cl = live[dev, pl.ds(2 * n + b, 1), :]
                        iv = inv[pl.ds(2 * n + b, 1), :]
                        pick = jnp.take_along_axis(words, (2 * n + b) * 4 + (lane >> 5), axis=1)
                        hit = jnp.left_shift(pick, up) < 0
                        t = jnp.tanh(0.5 * s[r0 : r0 + HALF, b * 128 : (b + 1) * 128])
                        g = t * cl + cl - jnp.where(hit, iv, 0.0)
                        sg[k, r0 : r0 + HALF, pl.ds(pl.multiple_of(n * WIDE + b * 128, 128), 128)] = g.astype(BF16)

        loop(body)

    def s1_copy(c, d, m, n):
        return remote(
            s1s.at[c, d, m, n], s1r.at[c, d, m, n], s1_ss.at[c, d, m, n], s1_rs.at[c, d, m, n], fast(c, 1 - 2 * d)
        )

    def query_chunk(k):
        def body(n):
            out = jnp.dot(sg[k], w_ref[:, tile_of(n)], preferred_element_type=F32)
            out = out.reshape(2, SIDE, HALF, WIDE)
            low, high = out[:, :, :QUART], out[:, :, QUART:]
            if k == 0:
                p0[n] = out
            for c in (0, 1):
                if k == 2:
                    s1s[c, 0, 0, n] = low[c].astype(BF16)
                    s1s[c, 1, 0, n] = high[c].astype(BF16)
                if k == 1:
                    p1[n, c] = low[c]
                    s1s[c, 0, 1, n] = high[c].astype(BF16)
                if k == 3:
                    p3[n, c] = high[c]
                    s1s[c, 1, 1, n] = low[c].astype(BF16)
            for c in (0, 1):
                if k in (1, 2):
                    s1_copy(c, 0, 2 - k, n).start()
                if k in (3, 2):
                    s1_copy(c, 1, 1 if k == 3 else 0, n).start()

        loop(body)

    def weight_tile(n, ks):
        out = None
        for k in ks:
            one = lax.dot_general(
                sg[k, :, tile_of(n)], q_all[k].reshape(rows_all, dim),
                (((0,), (0,)), ((), ())), preferred_element_type=F32,
            )
            out = one if out is None else out + one
        return out.reshape(2, RING, 2, 8, dim)

    def weight_first(n):
        wg[pl.ds(2 * n, 2)] = weight_tile(n, (0,))

    def x_copy(n):
        rows = pl.ds(2 * n, 2)
        return remote(wg.at[rows, :, 1 - core], xr.at[rows], x_ss.at[n], x_rs.at[n], other)

    def weight_last(n):
        rows = pl.ds(2 * n, 2)
        wg[rows] = wg[rows] + weight_tile(n, (3, 1, 2))
        x_copy(n).start()

    score_chunk(0)
    for c in (0, 1):
        p2b(c, 0)
    query_chunk(0)
    for c in (0, 1):
        p2b(c, 3)
        p2b(c, 1)
    loop(weight_first)
    for c in (0, 1):
        p2b(c, 2)
    score_chunk(3)
    query_chunk(3)
    score_chunk(1)
    query_chunk(1)
    for c in (0, 1):
        for j in range(SIDE):
            ag[c, j, 2].wait_recv()
            ag[c, j, 3].wait_recv()
    score_chunk(2)
    query_chunk(2)
    loop(weight_last)

    def z_copy(d, t, h):
        src, dst = (zs.at[d, t, h], zr.at[d, t, h]) if t < 3 else (zfs.at[d, h], zfr.at[d, h])
        return remote(src, dst, z_ss.at[d, t, h], z_rs.at[d, t, h], zdev(1 - 2 * d))

    def piece(r, h):
        i = lax.rem(z + r, RING)
        rows = slice(4 * h, 4 * h + 4)
        return (wg[rows, i, core] + xr[rows, i]).reshape(QUART, dim)

    def z_step(d, t, h):
        value = piece(4 - t if d == 0 else 4 + t, h)
        if t > (h if d == 0 else 1 - h):
            z_copy(d, t - 1, h).wait_recv()
            value = value + zr[d, t - 1, h].astype(F32)
        if t < 3:
            zs[d, t, h] = value.astype(BF16)
        else:
            zfs[d, h] = value
        go(z_copy(d, t, h))

    def s1_mid(n):
        for c in (0, 1):
            for d, keep in ((0, p1), (1, p3)):
                s1_copy(c, d, 0, n).wait_recv()
                s1s[c, d, 2, n] = (keep[n, c] + s1r[c, d, 0, n].astype(F32)).astype(BF16)
                go(s1_copy(c, d, 2, n))

    def s2_copy(c, d, n):
        return remote(s2s.at[c, d, n], s2r.at[c, d, n], s2_ss.at[c, d, 0, n], s2_rs.at[c, d, 0, n], slow(c, 1 - 2 * d))

    def s3_copy(c, d, n):
        return remote(s3s.at[c, d, n], s3r.at[c, d, n], s2_ss.at[c, d, 1, n], s2_rs.at[c, d, 1, n], slow(c, 1 - 2 * d))

    def s1_end(n):
        for c in (0, 1):
            for d in (0, 1):
                s1_copy(c, d, 1, n).wait_recv()
                s1_copy(c, d, 2, n).wait_recv()
            low = p0[n, c, :, :QUART] + s1r[c, 1, 1, n].astype(F32) + s1r[c, 0, 2, n].astype(F32)
            high = p0[n, c, :, QUART:] + s1r[c, 0, 1, n].astype(F32) + s1r[c, 1, 2, n].astype(F32)
            s2s[c, 0, n, 0] = low[2].astype(BF16)
            s2s[c, 0, n, 1] = high[1].astype(BF16)
            go(s2_copy(c, 0, n))
            s2s[c, 1, n, 0] = high[2].astype(BF16)
            s2s[c, 1, n, 1] = low[3].astype(BF16)
            go(s2_copy(c, 1, n))
            p0[n, c, 0, :QUART] = low[0]
            p0[n, c, 0, QUART:] = high[0]
            p1[n, c, 0] = low[1]
            p3[n, c, 0] = high[3]

    def s2_mid(n):
        for c in (0, 1):
            for d, keep in ((0, p1), (1, p3)):
                s2_copy(c, d, n).wait_recv()
                s3s[c, d, n] = keep[n, c, 0] + s2r[c, d, n, 0].astype(F32)
                go(s3_copy(c, d, n))

    def s2_end(n):
        cols = slice(n * WIDE, (n + 1) * WIDE)
        for c in (0, 1):
            s3_copy(c, 0, n).wait_recv()
            s3_copy(c, 1, n).wait_recv()
            qg_ref[c, :QUART, cols] = p0[n, c, 0, :QUART] + s2r[c, 1, n, 1].astype(F32) + s3r[c, 0, n]
            qg_ref[c, QUART:, cols] = p0[n, c, 0, QUART:] + s2r[c, 0, n, 1].astype(F32) + s3r[c, 1, n]

    for n in range(TILES):
        x_copy(n).wait_recv()
    z_step(0, 0, 0)
    z_step(1, 0, 1)
    z_step(0, 1, 1)
    z_step(1, 1, 0)
    s1_mid(0)
    s1_mid(1)
    z_step(0, 1, 0)
    z_step(1, 1, 1)
    s1_mid(2)
    s1_mid(3)
    z_step(0, 2, 1)
    z_step(1, 2, 0)
    s1_end(0)
    z_step(0, 2, 0)
    z_step(1, 2, 1)
    s1_end(1)
    z_step(0, 3, 1)
    z_step(1, 3, 0)
    s1_end(2)
    z_step(0, 3, 0)
    z_step(1, 3, 1)
    s1_end(3)
    for n in range(TILES):
        s2_mid(n)
    for n in range(TILES):
        s2_end(n)
    for h in (0, 1):
        z_copy(0, 3, h).wait_recv()
        z_copy(1, 3, h).wait_recv()
        wo_ref[4 * h : 4 * h + 4] = (piece(0, h) + zfr[0, h] + zfr[1, h]).reshape(4, 8, dim)
    for n in range(TILES):
        x_copy(n).wait_send()
        for c in (0, 1):
            for d in (0, 1):
                for m in (0, 1):
                    s1_copy(c, d, m, n).wait_send()
    for copy in started:
        copy.wait_send()


def per_device(queries, label_weights, propensity, positives, shortlist, owner_map):
    blocks, block_rows, dim = label_weights.shape
    hbm = pl.BlockSpec(memory_space=pl.ANY)
    vm = pl.BlockSpec(memory_space=pltpu.VMEM)
    dma = pltpu.SemaphoreType.DMA
    rows_all = 2 * SIDE * HALF
    qg, wo = pl.pallas_call(
        kernel,
        out_shape=(
            jax.ShapeDtypeStruct((2, HALF, dim), F32),
            jax.ShapeDtypeStruct((blocks, 8, dim), F32),
        ),
        in_specs=[hbm] * 6,
        out_specs=(vm, vm),
        scratch_shapes=[
            pltpu.VMEM((SIDE, 2, SIDE, HALF, dim), BF16),
            pltpu.VMEM((blocks * block_rows, dim), BF16),
            pltpu.VMEM((blocks, block_rows), F32),
            pltpu.VMEM((1, shortlist.shape[1]), I32),
            pltpu.VMEM((1, 128), I32),
            pltpu.VMEM((16, 128), I32),
            pltpu.VMEM((SIDE, SIDE, 16, 128), I32),
            pltpu.VMEM((SIDE * SIDE, 128, 128), I32),
            pltpu.VMEM((SIDE * SIDE, 8, 128), F32),
            pltpu.VMEM((8, 128), F32),
            pltpu.VMEM((SIDE, rows_all, blocks * block_rows), BF16),
            pltpu.VMEM((TILES, 2, SIDE, HALF, WIDE), F32),
            pltpu.VMEM((TILES, 2, SIDE, QUART, WIDE), F32),
            pltpu.VMEM((TILES, 2, SIDE, QUART, WIDE), F32),
            pltpu.VMEM((blocks, RING, 2, 8, dim), F32),
            pltpu.VMEM((2, 2, 3, TILES, SIDE, QUART, WIDE), BF16),
            pltpu.VMEM((2, 2, 3, TILES, SIDE, QUART, WIDE), BF16),
            pltpu.VMEM((2, 2, TILES, 2, QUART, WIDE), BF16),
            pltpu.VMEM((2, 2, TILES, 2, QUART, WIDE), BF16),
            pltpu.VMEM((2, 2, TILES, QUART, WIDE), F32),
            pltpu.VMEM((2, 2, TILES, QUART, WIDE), F32),
            pltpu.VMEM((blocks, RING, 8, dim), F32),
            pltpu.VMEM((2, 3, 2, QUART, dim), BF16),
            pltpu.VMEM((2, 3, 2, QUART, dim), BF16),
            pltpu.VMEM((2, 2, QUART, dim), F32),
            pltpu.VMEM((2, 2, QUART, dim), F32),
            dma((7,)),
            dma((2, 4)), dma((2, 4)),
            dma((2, 5, 4)), dma((2, 5, 4)),
            dma((2, 2, 3, TILES)), dma((2, 2, 3, TILES)),
            dma((2, 2, 2, TILES)), dma((2, 2, 2, TILES)),
            dma((TILES,)), dma((TILES,)),
            dma((2, 4, 2)), dma((2, 4, 2)),
        ],
        compiler_params=pltpu.CompilerParams(
            collective_id=0, has_side_effects=True, vmem_limit_bytes=60 * 1024 * 1024
        ),
    )(
        queries.reshape(2, HALF, dim),
        label_weights.reshape(blocks * block_rows, dim),
        propensity,
        positives.T,
        shortlist,
        owner_map.reshape(1, -1),
    )
    return qg.reshape(2 * HALF, dim), wo


def solution(mesh):
    in_specs = (
        P(("dp", "label", "section"), None),
        P("label", None, None),
        P("label", None),
        P(("dp", "label", "section"), None),
        P(("dp", "label"), None),
        P(),
    )
    out_specs = (P(("dp", "label", "section"), None), P("label", ("dp", "section"), None))
    return jax.shard_map(
        per_device, mesh=mesh, in_specs=in_specs, out_specs=out_specs, check_vma=False
    )
```

time: 89.7 us -> 72 us (0.80)
  Pallas kernels: 81.3 us -> 66.5 us
  other arithmetic: 3.6 us -> 0 us
    pallas_call x1, Pallas kernels: 81.3 us -> 66.5 us  [per_device(): pl.pallas_call(kernel, out_shape=(jax.ShapeDtypeStruct((2, HALF, dim), F3...]
    concatenate x1 -> x0, other arithmetic: 1.36 us -> none  [per_device(): jnp.concatenate([positives.T, entry_of[None, :], jnp.zeros((7, table), jn...]
    div x1 -> x0, other arithmetic: 1.29 us -> none  [per_device(): 1.0 / propensity]
    reduce_sum x2 -> x0, other arithmetic: 0.94 us -> none  [the longest x1 0.85 us: per_device(): stored = jnp.sum(jnp.where(lookup, owner_map[None, :], 0), axis=1)]
where the time goes in v2:
time: 72 us; the launch traced here: 70.7 us
  Pallas kernels  66.5 us (92%)
  local copies, waits for them, and re-layouts  3.56 us (5%)
    pallas_call x1, Pallas kernels, per_device(): pl.pallas_call(kernel, out_shape=(jax.ShapeDtypeStruct((2, HALF, dim), F3...  66.5 us
    unnamed x2, local copies, waits for them, and re-layouts  3.56 us

profile of v2, /device:TPU:32, one launch (start us, length us, event | category | flops | bytes accessed | tf_op | source)
XLA Modules:
  0.0 70.7 jit_solution(552958402625646585)
XLA Ops:
  0.6 66.5 %shard_map.77 = (f32[2,64,1024]{2,1,0:T(8,128)}, f32[8,8,1024]{2,1,0:T(8,128)}) custom-call(bf16[2,64,1024]{2,1,0:T(8,128)(2,1)} %bitcast.7, bf16[1024,1024]{1,0:T(8,128)(2,1)} %bitcast.5, f32[8,128]{1,0:T(8,128)} %prop_hbm.1, s32[8,128]{1,0:T(8,128)} %bitcast.8, s32[1,48]{1,0:T(1,128)} %list_hbm.1, s32[1,128]{1,0:T(1,128)} %bitcast.9), custom_call_target="tpu_custom_call" | custom-call | tf_op jit(solution)/shard_map/pallas_call | solution.py:394
  67.1 1.9 %copy.10 = f32[128,1024]{1,0:T(8,128)} copy(f32[128,1024]{1,0:T(8,128)} %bitcast.6) | data formatting | bytes 1048576
  69.0 1.7 %copy.11 = f32[8,8,1024]{2,1,0:T(8,128)} copy(f32[8,8,1024]{2,1,0:T(8,128)} %get-tuple-element.9) | data formatting | bytes 524288

commit v3 on v2

v3 whole, which is shorter than its diff:
```python
import jax
import jax.numpy as jnp
from jax import lax
from jax.experimental import pallas as pl
from jax.experimental.pallas import tpu as pltpu
from jax.sharding import PartitionSpec as P

MESH = pl.DeviceIdType.MESH
SIDE = 4
RING = 8
HALF = 64
QUART = 32
TILES = 4
WIDE = 256
FAR = 1 << 20
grad_scale = 0.25
F32, BF16, I32 = jnp.float32, jnp.bfloat16, jnp.int32


def kernel(
    q_hbm, w_hbm, prop_hbm, pos_hbm, list_hbm, map_hbm, qg_ref, wo_ref,
    q_all, w_ref, prop_ref, list_ref, map_ref, meta, meta_all, words_t, live, inv,
    sg, p0, p1, p3, wg, s1s, s1r, s2s, s2r, s3s, s3r, xr, zs, zr, zfs, zfr,
    loc_s, me_ss, me_rs, ag_ss, ag_rs, s1_ss, s1_rs, s2_ss, s2_rs, x_ss, x_rs, z_ss, z_rs,
):
    label = lax.axis_index("label")
    z = lax.axis_index("dp")
    core = lax.axis_index("section")
    x, y = label // SIDE, label % SIDE
    dim = SIDE * WIDE

    def at(dx, dy):
        return {"label": lax.rem(x + dx + SIDE, SIDE) * SIDE + lax.rem(y + dy + SIDE, SIDE)}

    def along(axis, d):
        return at(d, 0) if axis == 0 else at(0, d)

    def slow(c, d):
        return along(c, d)

    def fast(c, d):
        return along(1 - c, d)

    def zdev(d):
        return {"dp": lax.rem(z + d + RING, RING)}

    other = {"section": 1 - core}

    peers = [at(d, 0) for d in (1, 2, 3)] + [at(0, d) for d in (1, 2, 3)] + [zdev(1), zdev(-1), other]
    barrier = pltpu.get_barrier_semaphore()
    for peer in peers:
        pl.semaphore_signal(barrier, inc=1, device_id=peer, device_id_type=MESH)

    def local(i, src, dst):
        copy = pltpu.make_async_copy(src, dst, loc_s.at[i])
        copy.start()
        return copy

    loc_q = [local(c, q_hbm.at[c], q_all.at[c]) for c in (0, 1)]
    loc_m = [local(2, list_hbm, list_ref), local(3, map_hbm, map_ref), local(4, pos_hbm, meta.at[pl.ds(0, 8)])]
    loc_w = [local(5, w_hbm, w_ref), local(6, prop_hbm, prop_ref)]

    pl.semaphore_wait(barrier, len(peers))

    def remote(src, dst, ss, rs, dev):
        return pltpu.make_async_remote_copy(
            src_ref=src, dst_ref=dst, send_sem=ss, recv_sem=rs, device_id=dev, device_id_type=MESH
        )

    started = []

    def go(copy):
        copy.start()
        started.append(copy)
        return copy

    def blocks_of(ks, js):
        return [(k, c, j) for k in ks for j in js for c in (0, 1)]

    chunk_a = blocks_of((0,), (0, 3, 1))
    chunk_b = blocks_of((0,), (2,)) + blocks_of((3, 1), (0,))
    chunk_c = blocks_of((3, 1), (3, 1))
    chunk_d = blocks_of((3, 1), (2,))
    chunk_e = blocks_of((2,), (0, 3))
    chunk_f = blocks_of((2,), (1, 2))
    order = chunk_a + chunk_b + chunk_c + chunk_d + chunk_e + chunk_f

    def slot_of(k, c, j):
        return order.index((k, c, j))

    def qa(k, c, j, rows=None):
        ref = q_all.at[slot_of(k, c, j)]
        return ref if rows is None else ref.at[rows]

    lo, hi = pl.ds(0, QUART), pl.ds(QUART, QUART)
    ag = {}

    def ag_send(c, slot, kind, src, dst, dev):
        ag[c, slot, kind] = go(remote(src, dst, ag_ss.at[c, slot, kind], ag_rs.at[c, slot, kind], dev))

    def p1a(c):
        ag_send(c, 4, 0, qa(0, c, 0), qa(0, c, 3), slow(c, 1))
        ag_send(c, 4, 1, qa(0, c, 0), qa(0, c, 1), slow(c, -1))

    def p1b(c, kind):
        ag[c, 4, kind].wait_recv()
        if kind == 0:
            ag_send(c, 4, 2, qa(0, c, 3, lo), qa(0, c, 2, lo), slow(c, 1))
        else:
            ag_send(c, 4, 3, qa(0, c, 1, hi), qa(0, c, 2, hi), slow(c, -1))

    def p2a(c, j):
        ag_send(c, j, 0, qa(0, c, j), qa(3, c, j), fast(c, 1))
        ag_send(c, j, 1, qa(0, c, j), qa(1, c, j), fast(c, -1))

    def p2b(c, j):
        ag[c, j, 0].wait_recv()
        ag_send(c, j, 2, qa(3, c, j, lo), qa(2, c, j, lo), fast(c, 1))
        ag[c, j, 1].wait_recv()
        ag_send(c, j, 3, qa(1, c, j, hi), qa(2, c, j, hi), fast(c, -1))

    for copy in loc_q:
        copy.wait()
    p1a(0)
    p1a(1)

    for copy in loc_m:
        copy.wait()
    short = list_ref.shape[1]
    sub = lax.broadcasted_iota(I32, (short, short), 0)
    lane = lax.broadcasted_iota(I32, (short, short), 1)
    list_col = jnp.sum(jnp.where(sub == lane, list_ref[...], 0), axis=1, keepdims=True)
    sub = lax.broadcasted_iota(I32, (short, 128), 0)
    lane = lax.broadcasted_iota(I32, (short, 128), 1)
    stored = jnp.sum(jnp.where(list_col == lane, map_ref[...], 0), axis=1, keepdims=True)
    meta[pl.ds(8, 8), :] = jnp.broadcast_to(
        jnp.sum(jnp.where(stored == lane, sub + 1, 0), axis=0, keepdims=True) - 1, (8, 128)
    )
    meta_all[0, 0] = meta[...]

    meta_x = [go(remote(meta, meta_all.at[SIDE - a, 0], me_ss.at[0, a], me_rs.at[0, a], at(a, 0))) for a in (1, 3, 2)]
    meta_y = [go(remote(meta, meta_all.at[0, SIDE - a], me_ss.at[1, a], me_rs.at[1, a], at(0, a))) for a in (1, 3, 2)]
    p2a(0, 0)
    p2a(1, 0)
    words_t[...] = jnp.zeros_like(words_t)
    for copy in loc_w:
        copy.wait()
    inv[...] = grad_scale / prop_ref[...]
    for c in (0, 1):
        p1b(c, 0)
        p1b(c, 1)
    for copy in meta_x:
        copy.wait_recv()
    far = pl.ds(1, SIDE - 1)
    meta_xy = [
        go(remote(meta_all.at[far, 0], meta_all.at[far, SIDE - a], me_ss.at[2, a], me_rs.at[2, a], at(0, a)))
        for a in (1, 3, 2)
    ]
    for c in (0, 1):
        p2a(c, 3)
        p2a(c, 1)
    for copy in meta_y:
        copy.wait_recv()

    def prepare(d):
        tile = meta_all[d // SIDE, d % SIDE]
        sub = lax.broadcasted_iota(I32, (QUART, 128), 0)
        lane = lax.broadcasted_iota(I32, (QUART, 128), 1)
        row = tile[8:9, :]
        entry = jnp.sum(jnp.where(lane == label * 8 + sub // 4, row, 0), axis=1, keepdims=True)
        base = jnp.where(entry >= 0, entry * 128 + (sub % 4) * 32, FAR)
        words = jnp.zeros((QUART, 128), I32)
        for p in range(8):
            rel = tile[p : p + 1, :] - base
            words = words | jnp.where((rel >= 0) & (rel < 32), jnp.left_shift(1, rel & 31), 0)
        words_t[d, :, 0:QUART] = jnp.transpose(words)
        sub8 = lax.broadcasted_iota(I32, (8, 128), 0)
        lane8 = lax.broadcasted_iota(I32, (8, 128), 1)
        entry8 = jnp.sum(jnp.where(lane8 == label * 8 + sub8, row, 0), axis=1, keepdims=True)
        live[d] = jnp.broadcast_to(jnp.where(entry8 >= 0, 0.5 * grad_scale, 0.0), (8, 128))

    for d in range(SIDE * SIDE):
        if d < SIDE or d % SIDE == 0:
            prepare(d)

    def tile_of(n):
        return pl.ds(n * WIDE, WIDE)

    def loop(body):
        for n in range(TILES):
            body(n)

    def rows_of(group):
        return pl.ds(slot_of(*group[0]) * HALF, len(group) * HALF)

    def queries_of(group):
        first = slot_of(*group[0])
        return q_all[first : first + len(group)].reshape(len(group) * HALF, dim)

    def score_chunk(group):
        first = slot_of(*group[0])

        def body(n):
            s = lax.dot_general(
                queries_of(group), w_ref[tile_of(n), :], (((1,), (1,)), ((), ())), preferred_element_type=F32
            )
            lane = lax.broadcasted_iota(I32, (HALF, 128), 1)
            up = 31 - (lane & 31)
            for i, (k, c, j) in enumerate(group):
                dev = j * SIDE + k if c == 0 else k * SIDE + j
                r0 = i * HALF
                words = words_t[dev, c * HALF : (c + 1) * HALF, :]
                for b in (0, 1):
                    cl = live[dev, pl.ds(2 * n + b, 1), :]
                    iv = inv[pl.ds(2 * n + b, 1), :]
                    pick = jnp.take_along_axis(words, (2 * n + b) * 4 + (lane >> 5), axis=1)
                    hit = jnp.left_shift(pick, up) < 0
                    t = jnp.tanh(0.5 * s[r0 : r0 + HALF, b * 128 : (b + 1) * 128])
                    g = t * cl + cl - jnp.where(hit, iv, 0.0)
                    cols = pl.ds(n * WIDE + b * 128, 128)
                    sg[pl.ds((first + i) * HALF, HALF), cols] = g.astype(BF16)

        loop(body)

    def s1_copy(c, d, m, n):
        return remote(
            s1s.at[c, d, m, n], s1r.at[c, d, m, n], s1_ss.at[c, d, m, n], s1_rs.at[c, d, m, n], fast(c, 1 - 2 * d)
        )

    def query_chunk(group, send):
        def body(n):
            out = jnp.dot(sg[rows_of(group), :], w_ref[:, tile_of(n)], preferred_element_type=F32)
            for i, (k, c, j) in enumerate(group):
                low, high = out[i * HALF : i * HALF + QUART], out[i * HALF + QUART : (i + 1) * HALF]
                if k == 0:
                    p0[n, c, j] = out[i * HALF : (i + 1) * HALF]
                if k == 2:
                    s1s[c, 0, 0, n, j] = low.astype(BF16)
                    s1s[c, 1, 0, n, j] = high.astype(BF16)
                if k == 1:
                    p1[n, c, j] = low
                    s1s[c, 0, 1, n, j] = high.astype(BF16)
                if k == 3:
                    p3[n, c, j] = high
                    s1s[c, 1, 1, n, j] = low.astype(BF16)
            if send is not None:
                for c in (0, 1):
                    for d in (0, 1):
                        s1_copy(c, d, send, n).start()

        loop(body)

    def weight_tile(n, group):
        return lax.dot_general(
            sg[rows_of(group), tile_of(n)], queries_of(group),
            (((0,), (0,)), ((), ())), preferred_element_type=F32,
        ).reshape(2, RING, 2, 8, dim)

    def x_copy(n):
        rows = pl.ds(2 * n, 2)
        return remote(wg.at[rows, :, 1 - core], xr.at[rows], x_ss.at[n], x_rs.at[n], other)

    def weight_chunk(group):
        def body(n):
            rows = pl.ds(2 * n, 2)
            if group[0] == chunk_a[0]:
                wg[rows] = weight_tile(n, group)
            else:
                wg[rows] = wg[rows] + weight_tile(n, group)
            if group[-1] == chunk_f[-1]:
                x_copy(n).start()

        loop(body)

    score_chunk(chunk_a)
    query_chunk(chunk_a, None)
    for copy in meta_xy:
        copy.wait_recv()
    for d in range(SIDE * SIDE):
        if d >= SIDE and d % SIDE:
            prepare(d)
    for c in (0, 1):
        ag[c, 4, 2].wait_recv()
        ag[c, 4, 3].wait_recv()
        p2a(c, 2)
    for c in (0, 1):
        p2b(c, 0)
    score_chunk(chunk_b)
    query_chunk(chunk_b, None)
    for c in (0, 1):
        p2b(c, 3)
    weight_chunk(chunk_a + chunk_b)
    for c in (0, 1):
        p2b(c, 1)
    score_chunk(chunk_c)
    query_chunk(chunk_c, None)
    for c in (0, 1):
        p2b(c, 2)
    score_chunk(chunk_d)
    query_chunk(chunk_d, 1)
    weight_chunk(chunk_c + chunk_d)
    for j in (0, 3):
        for c in (0, 1):
            ag[c, j, 2].wait_recv()
            ag[c, j, 3].wait_recv()
    score_chunk(chunk_e)
    query_chunk(chunk_e, None)
    for j in (1, 2):
        for c in (0, 1):
            ag[c, j, 2].wait_recv()
            ag[c, j, 3].wait_recv()
    score_chunk(chunk_f)
    query_chunk(chunk_f, 0)
    weight_chunk(chunk_e + chunk_f)

    def z_copy(d, t, n):
        sem = (z_ss.at[d, t, n], z_rs.at[d, t, n], zdev(1 - 2 * d))
        if t == 0:
            return remote(zs.at[d, 2, n, pl.ds(0, 8)], zr.at[d, 2, n, pl.ds(0, 8)], *sem)
        if t < 3:
            return remote(zs.at[d, t - 1, n], zr.at[d, t - 1, n], *sem)
        return remote(zfs.at[d, n], zfr.at[d, n], *sem)

    def piece(r, n):
        i = lax.rem(z + r, RING)
        rows = slice(2 * n, 2 * n + 2)
        return wg[rows, i, core] + xr[rows, i]

    def z_step(d, t, n):
        if t == 0:
            i = lax.rem(z + 4, RING)
            zs[d, 2, n, 0:8] = (wg[2 * n + d, i, core] + xr[2 * n + d, i]).astype(BF16)
        else:
            value = piece(4 - t if d == 0 else 4 + t, n)
            z_copy(d, t - 1, n).wait_recv()
            if t == 1:
                came = zr[d, 2, n, 0:8].astype(F32)
                none = jnp.zeros_like(came)
                value = value + jnp.stack([came, none] if d == 0 else [none, came])
            else:
                value = value + zr[d, t - 2, n].astype(F32).reshape(2, 8, dim)
            value = value.reshape(16, dim)
            if t < 3:
                zs[d, t - 1, n] = value.astype(BF16)
            else:
                zfs[d, n] = value
        go(z_copy(d, t, n))

    def z_hop(t, n):
        z_step(0, t, n)
        z_step(1, t, n)

    def s1_mid(n):
        for c in (0, 1):
            for d, keep in ((0, p1), (1, p3)):
                s1_copy(c, d, 0, n).wait_recv()
                s1s[c, d, 2, n] = (keep[n, c] + s1r[c, d, 0, n].astype(F32)).astype(BF16)
                go(s1_copy(c, d, 2, n))

    def s2_copy(c, d, n):
        return remote(s2s.at[c, d, n], s2r.at[c, d, n], s2_ss.at[c, d, 0, n], s2_rs.at[c, d, 0, n], slow(c, 1 - 2 * d))

    def s3_copy(c, d, n):
        return remote(s3s.at[c, d, n], s3r.at[c, d, n], s2_ss.at[c, d, 1, n], s2_rs.at[c, d, 1, n], slow(c, 1 - 2 * d))

    def s1_end(n):
        for c in (0, 1):
            for d in (0, 1):
                s1_copy(c, d, 1, n).wait_recv()
                s1_copy(c, d, 2, n).wait_recv()
            low = p0[n, c, :, :QUART] + s1r[c, 1, 1, n].astype(F32) + s1r[c, 0, 2, n].astype(F32)
            high = p0[n, c, :, QUART:] + s1r[c, 0, 1, n].astype(F32) + s1r[c, 1, 2, n].astype(F32)
            s2s[c, 0, n, 0] = low[2].astype(BF16)
            s2s[c, 0, n, 1] = high[1].astype(BF16)
            go(s2_copy(c, 0, n))
            s2s[c, 1, n, 0] = high[2].astype(BF16)
            s2s[c, 1, n, 1] = low[3].astype(BF16)
            go(s2_copy(c, 1, n))
            p0[n, c, 0, :QUART] = low[0]
            p0[n, c, 0, QUART:] = high[0]
            p1[n, c, 0] = low[1]
            p3[n, c, 0] = high[3]

    def s2_mid(n):
        for c in (0, 1):
            for d, keep in ((0, p1), (1, p3)):
                s2_copy(c, d, n).wait_recv()
                s3s[c, d, n] = keep[n, c, 0] + s2r[c, d, n, 0].astype(F32)
                go(s3_copy(c, d, n))

    def s2_end(n):
        cols = slice(n * WIDE, (n + 1) * WIDE)
        for c in (0, 1):
            s3_copy(c, 0, n).wait_recv()
            s3_copy(c, 1, n).wait_recv()
            qg_ref[c, :QUART, cols] = p0[n, c, 0, :QUART] + s2r[c, 1, n, 1].astype(F32) + s3r[c, 0, n]
            qg_ref[c, QUART:, cols] = p0[n, c, 0, QUART:] + s2r[c, 0, n, 1].astype(F32) + s3r[c, 1, n]

    for n in range(TILES):
        x_copy(n).wait_recv()
        z_hop(0, n)
    s1_mid(0)
    s1_mid(1)
    for n in range(TILES):
        z_hop(1, n)
    s1_mid(2)
    s1_mid(3)
    z_hop(2, 0)
    z_hop(2, 1)
    s1_end(0)
    z_hop(2, 2)
    z_hop(2, 3)
    s1_end(1)
    z_hop(3, 0)
    z_hop(3, 1)
    s1_end(2)
    z_hop(3, 2)
    z_hop(3, 3)
    s1_end(3)
    for n in range(TILES):
        s2_mid(n)
    for n in range(TILES):
        s2_end(n)
    for n in range(TILES):
        z_copy(0, 3, n).wait_recv()
        z_copy(1, 3, n).wait_recv()
        wo_ref[2 * n : 2 * n + 2] = piece(0, n) + (zfr[0, n] + zfr[1, n]).reshape(2, 8, dim)
    for n in range(TILES):
        x_copy(n).wait_send()
        for c in (0, 1):
            for d in (0, 1):
                for m in (0, 1):
                    s1_copy(c, d, m, n).wait_send()
    for copy in started:
        copy.wait_send()


def per_device(queries, label_weights, propensity, positives, shortlist, owner_map):
    blocks, block_rows, dim = label_weights.shape
    hbm = pl.BlockSpec(memory_space=pl.ANY)
    vm = pl.BlockSpec(memory_space=pltpu.VMEM)
    dma = pltpu.SemaphoreType.DMA
    qg, wo = pl.pallas_call(
        kernel,
        out_shape=(
            pltpu.VMEM((2, HALF, dim), F32),
            pltpu.VMEM((blocks, 8, dim), F32),
        ),
        in_specs=[hbm] * 6,
        out_specs=(vm, vm),
        scratch_shapes=[
            pltpu.VMEM((SIDE * 2 * SIDE, HALF, dim), BF16),
            pltpu.VMEM((blocks * block_rows, dim), BF16),
            pltpu.VMEM((blocks, block_rows), F32),
            pltpu.VMEM((1, shortlist.shape[1]), I32),
            pltpu.VMEM((1, 128), I32),
            pltpu.VMEM((16, 128), I32),
            pltpu.VMEM((SIDE, SIDE, 16, 128), I32),
            pltpu.VMEM((SIDE * SIDE, 128, 128), I32),
            pltpu.VMEM((SIDE * SIDE, 8, 128), F32),
            pltpu.VMEM((8, 128), F32),
            pltpu.VMEM((SIDE * 2 * SIDE * HALF, blocks * block_rows), BF16),
            pltpu.VMEM((TILES, 2, SIDE, HALF, WIDE), F32),
            pltpu.VMEM((TILES, 2, SIDE, QUART, WIDE), F32),
            pltpu.VMEM((TILES, 2, SIDE, QUART, WIDE), F32),
            pltpu.VMEM((blocks, RING, 2, 8, dim), F32),
            pltpu.VMEM((2, 2, 3, TILES, SIDE, QUART, WIDE), BF16),
            pltpu.VMEM((2, 2, 3, TILES, SIDE, QUART, WIDE), BF16),
            pltpu.VMEM((2, 2, TILES, 2, QUART, WIDE), BF16),
            pltpu.VMEM((2, 2, TILES, 2, QUART, WIDE), BF16),
            pltpu.VMEM((2, 2, TILES, QUART, WIDE), F32),
            pltpu.VMEM((2, 2, TILES, QUART, WIDE), F32),
            pltpu.VMEM((blocks, RING, 8, dim), F32),
            pltpu.VMEM((2, 3, TILES, 16, dim), BF16),
            pltpu.VMEM((2, 3, TILES, 16, dim), BF16),
            pltpu.VMEM((2, TILES, 16, dim), F32),
            pltpu.VMEM((2, TILES, 16, dim), F32),
            dma((7,)),
            dma((3, 4)), dma((3, 4)),
            dma((2, 5, 4)), dma((2, 5, 4)),
            dma((2, 2, 3, TILES)), dma((2, 2, 3, TILES)),
            dma((2, 2, 2, TILES)), dma((2, 2, 2, TILES)),
            dma((TILES,)), dma((TILES,)),
            dma((2, 4, TILES)), dma((2, 4, TILES)),
        ],
        compiler_params=pltpu.CompilerParams(
            collective_id=0, has_side_effects=True, vmem_limit_bytes=66_256_896
        ),
    )(
        queries.reshape(2, HALF, dim),
        label_weights.reshape(blocks * block_rows, dim),
        propensity,
        positives.T,
        shortlist,
        owner_map.reshape(1, -1),
    )
    return qg.reshape(2 * HALF, dim), wo


def solution(mesh):
    in_specs = (
        P(("dp", "label", "section"), None),
        P("label", None, None),
        P("label", None),
        P(("dp", "label", "section"), None),
        P(("dp", "label"), None),
        P(),
    )
    out_specs = (P(("dp", "label", "section"), None), P("label", ("dp", "section"), None))
    return jax.shard_map(
        per_device, mesh=mesh, in_specs=in_specs, out_specs=out_specs, check_vma=False
    )
```

time: 72 us -> 63.6 us (0.88); the launches traced: 70.7 us -> 63.5 us
  Pallas kernels: 66.5 us -> 61.4 us
  local copies, waits for them, and re-layouts: 3.56 us -> 1.5 us
    pallas_call x1, Pallas kernels: 66.5 us -> 61.4 us  [per_device(): pl.pallas_call(kernel, out_shape=(pltpu.VMEM((2, HALF, dim), F32), pltpu....]
    unnamed x2, local copies, waits for them, and re-layouts: 3.56 us -> 1.5 us
where the time goes in v3:
time: 63.6 us; the launch traced here: 63.5 us
  Pallas kernels  61.4 us (97%)
  local copies, waits for them, and re-layouts  1.5 us (2%)
  between operations  0.64 us (1%)
    pallas_call x1, Pallas kernels, per_device(): pl.pallas_call(kernel, out_shape=(pltpu.VMEM((2, HALF, dim), F32), pltpu....  61.4 us
    unnamed x2, local copies, waits for them, and re-layouts  1.5 us

profile of v3, /device:TPU:32, one launch (start us, length us, event | category | flops | bytes accessed | tf_op | source)
XLA Modules:
  0.0 63.5 jit_solution(14721891885957881611)
XLA Ops:
  0.6 61.4 %shard_map.77 = (f32[2,64,1024]{2,1,0:T(8,128)S(1)}, f32[8,8,1024]{2,1,0:T(8,128)S(1)}) custom-call(bf16[2,64,1024]{2,1,0:T(8,128)(2,1)} %bitcast.7, bf16[1024,1024]{1,0:T(8,128)(2,1)} %bitcast.6, f32[8,128]{1,0:T(8,128)} %prop_hbm.1, s32[8,128]{1,0:T(8,128)} %bitcast.8, s32[1,48]{1,0:T(1,128)} %list_hbm.1, s32[1,128]{1,0:T(1,128)} %bitcast.9), custom_call_target="tpu_custom_call" | custom-call | tf_op jit(solution)/shard_map/pallas_call | solution.py:443
  62.0 0.8 %copy.10 = f32[128,1024]{1,0:T(8,128)} copy(f32[128,1024]{1,0:T(8,128)S(1)} %bitcast.5) | data formatting | bytes 1048576
  62.8 0.7 %copy.11 = f32[8,8,1024]{2,1,0:T(8,128)} copy(f32[8,8,1024]{2,1,0:T(8,128)S(1)} %get-tuple-element.7) | data formatting | bytes 524288

commit v4 on v3

--- a/solution.py
+++ b/solution.py
@@ -21,7 +21,7 @@
     q_hbm, w_hbm, prop_hbm, pos_hbm, list_hbm, map_hbm, qg_ref, wo_ref,
     q_all, w_ref, prop_ref, list_ref, map_ref, meta, meta_all, words_t, live, inv,
     sg, p0, p1, p3, wg, s1s, s1r, s2s, s2r, s3s, s3r, xr, zs, zr, zfs, zfr,
-    loc_s, me_ss, me_rs, ag_ss, ag_rs, s1_ss, s1_rs, s2_ss, s2_rs, x_ss, x_rs, z_ss, z_rs,
+    loc_s, me_ss, me_rs, ag_ss, ag_rs, s1_ss, s1_rs, s2_ss, s2_rs, x_ss, x_rs, z_ss, z_rs, met,
 ):
     label = lax.axis_index("label")
     z = lax.axis_index("dp")
@@ -46,10 +46,17 @@
 
     other = {"section": 1 - core}
 
-    peers = [at(d, 0) for d in (1, 2, 3)] + [at(0, d) for d in (1, 2, 3)] + [zdev(1), zdev(-1), other]
+    peers = [at(d, 0) for d in (1, 2, 3)] + [at(0, d) for d in (1, 2, 3)] + [other]
+    odd = lax.rem(z, 2)
     barrier = pltpu.get_barrier_semaphore()
     for peer in peers:
         pl.semaphore_signal(barrier, inc=1, device_id=peer, device_id_type=MESH)
+
+    @pl.when(odd == 0)
+    def _():
+        for d in (1, -1):
+            pl.semaphore_signal(barrier, inc=1, device_id=zdev(d), device_id_type=MESH)
+
 
     def local(i, src, dst):
         copy = pltpu.make_async_copy(src, dst, loc_s.at[i])
@@ -59,70 +66,6 @@
     loc_q = [local(c, q_hbm.at[c], q_all.at[c]) for c in (0, 1)]
     loc_m = [local(2, list_hbm, list_ref), local(3, map_hbm, map_ref), local(4, pos_hbm, meta.at[pl.ds(0, 8)])]
     loc_w = [local(5, w_hbm, w_ref), local(6, prop_hbm, prop_ref)]
-
-    pl.semaphore_wait(barrier, len(peers))
-
-    def remote(src, dst, ss, rs, dev):
-        return pltpu.make_async_remote_copy(
-            src_ref=src, dst_ref=dst, send_sem=ss, recv_sem=rs, device_id=dev, device_id_type=MESH
-        )
-
-    started = []
-
-    def go(copy):
-        copy.start()
-        started.append(copy)
-        return copy
-
-    def blocks_of(ks, js):
-        return [(k, c, j) for k in ks for j in js for c in (0, 1)]
-
-    chunk_a = blocks_of((0,), (0, 3, 1))
-    chunk_b = blocks_of((0,), (2,)) + blocks_of((3, 1), (0,))
-    chunk_c = blocks_of((3, 1), (3, 1))
-    chunk_d = blocks_of((3, 1), (2,))
-    chunk_e = blocks_of((2,), (0, 3))
-    chunk_f = blocks_of((2,), (1, 2))
-    order = chunk_a + chunk_b + chunk_c + chunk_d + chunk_e + chunk_f
-
-    def slot_of(k, c, j):
-        return order.index((k, c, j))
-
-    def qa(k, c, j, rows=None):
-        ref = q_all.at[slot_of(k, c, j)]
-        return ref if rows is None else ref.at[rows]
-
-    lo, hi = pl.ds(0, QUART), pl.ds(QUART, QUART)
-    ag = {}
-
-    def ag_send(c, slot, kind, src, dst, dev):
-        ag[c, slot, kind] = go(remote(src, dst, ag_ss.at[c, slot, kind], ag_rs.at[c, slot, kind], dev))
-
-    def p1a(c):
-        ag_send(c, 4, 0, qa(0, c, 0), qa(0, c, 3), slow(c, 1))
-        ag_send(c, 4, 1, qa(0, c, 0), qa(0, c, 1), slow(c, -1))
-
-    def p1b(c, kind):
-        ag[c, 4, kind].wait_recv()
-        if kind == 0:
-            ag_send(c, 4, 2, qa(0, c, 3, lo), qa(0, c, 2, lo), slow(c, 1))
-        else:
-            ag_send(c, 4, 3, qa(0, c, 1, hi), qa(0, c, 2, hi), slow(c, -1))
-
-    def p2a(c, j):
-        ag_send(c, j, 0, qa(0, c, j), qa(3, c, j), fast(c, 1))
-        ag_send(c, j, 1, qa(0, c, j), qa(1, c, j), fast(c, -1))
-
-    def p2b(c, j):
-        ag[c, j, 0].wait_recv()
-        ag_send(c, j, 2, qa(3, c, j, lo), qa(2, c, j, lo), fast(c, 1))
-        ag[c, j, 1].wait_recv()
-        ag_send(c, j, 3, qa(1, c, j, hi), qa(2, c, j, hi), fast(c, -1))
-
-    for copy in loc_q:
-        copy.wait()
-    p1a(0)
-    p1a(1)
 
     for copy in loc_m:
         copy.wait()
@@ -138,17 +81,84 @@
     )
     meta_all[0, 0] = meta[...]
 
+    pl.semaphore_wait(barrier, len(peers) + 2 * odd)
+
+    @pl.when(odd == 1)
+    def _():
+        for d in (1, -1):
+            pl.semaphore_signal(met, inc=1, device_id=zdev(d), device_id_type=MESH)
+
+
+    def remote(src, dst, ss, rs, dev):
+        return pltpu.make_async_remote_copy(
+            src_ref=src, dst_ref=dst, send_sem=ss, recv_sem=rs, device_id=dev, device_id_type=MESH
+        )
+
+    started = []
+
+    def go(copy):
+        copy.start()
+        started.append(copy)
+        return copy
+
+    def blocks_of(ks, js):
+        return [(k, c, j) for k in ks for j in js for c in (0, 1)]
+
+    chunk_a = blocks_of((0,), (0, 3, 1))
+    chunk_b = blocks_of((0,), (2,)) + blocks_of((3, 1), (0,))
+    chunk_c = blocks_of((3, 1), (3, 1))
+    chunk_d = blocks_of((3, 1), (2,))
+    chunk_e = blocks_of((2,), (0, 3))
+    chunk_f = blocks_of((2,), (1, 2))
+    order = chunk_a + chunk_b + chunk_c + chunk_d + chunk_e + chunk_f
+
+    def slot_of(k, c, j):
+        return order.index((k, c, j))
+
+    def qa(k, c, j, rows=None):
+        ref = q_all.at[slot_of(k, c, j)]
+        return ref if rows is None else ref.at[rows]
+
+    lo, hi = pl.ds(0, QUART), pl.ds(QUART, QUART)
+    ag = {}
+
+    def ag_send(c, slot, kind, src, dst, dev):
+        ag[c, slot, kind] = go(remote(src, dst, ag_ss.at[c, slot, kind], ag_rs.at[c, slot, kind], dev))
+
+    def p1a(c, slot):
+        up, down = (lo, hi) if slot == 4 else (hi, lo)
+        ag_send(c, slot, 0, qa(0, c, 0, up), qa(0, c, 3, up), slow(c, 1))
+        ag_send(c, slot, 1, qa(0, c, 0, down), qa(0, c, 1, down), slow(c, -1))
+
+    def p1b(c, kind):
+        ag[c, 4, kind].wait_recv()
+        if kind == 0:
+            ag_send(c, 4, 2, qa(0, c, 3, lo), qa(0, c, 2, lo), slow(c, 1))
+        else:
+            ag_send(c, 4, 3, qa(0, c, 1, hi), qa(0, c, 2, hi), slow(c, -1))
+
+    def p2a(c, j):
+        ag_send(c, j, 0, qa(0, c, j), qa(3, c, j), fast(c, 1))
+        ag_send(c, j, 1, qa(0, c, j), qa(1, c, j), fast(c, -1))
+
+    def p2b(c, j):
+        ag[c, j, 0].wait_recv()
+        ag_send(c, j, 2, qa(3, c, j, lo), qa(2, c, j, lo), fast(c, 1))
+        ag[c, j, 1].wait_recv()
+        ag_send(c, j, 3, qa(1, c, j, hi), qa(2, c, j, hi), fast(c, -1))
+
     meta_x = [go(remote(meta, meta_all.at[SIDE - a, 0], me_ss.at[0, a], me_rs.at[0, a], at(a, 0))) for a in (1, 3, 2)]
     meta_y = [go(remote(meta, meta_all.at[0, SIDE - a], me_ss.at[1, a], me_rs.at[1, a], at(0, a))) for a in (1, 3, 2)]
-    p2a(0, 0)
-    p2a(1, 0)
+    for copy in loc_q:
+        copy.wait()
+    p1a(0, 4)
+    p1a(1, 4)
+    p1a(0, 5)
+    p1a(1, 5)
     words_t[...] = jnp.zeros_like(words_t)
     for copy in loc_w:
         copy.wait()
     inv[...] = grad_scale / prop_ref[...]
-    for c in (0, 1):
-        p1b(c, 0)
-        p1b(c, 1)
     for copy in meta_x:
         copy.wait_recv()
     far = pl.ds(1, SIDE - 1)
@@ -157,8 +167,10 @@
         for a in (1, 3, 2)
     ]
     for c in (0, 1):
-        p2a(c, 3)
-        p2a(c, 1)
+        p1b(c, 0)
+        p1b(c, 1)
+    p2a(0, 0)
+    p2a(1, 0)
     for copy in meta_y:
         copy.wait_recv()
 
@@ -182,6 +194,11 @@
     for d in range(SIDE * SIDE):
         if d < SIDE or d % SIDE == 0:
             prepare(d)
+    for c in (0, 1):
+        ag[c, 5, 0].wait_recv()
+        ag[c, 5, 1].wait_recv()
+        p2a(c, 3)
+        p2a(c, 1)
 
     def tile_of(n):
         return pl.ds(n * WIDE, WIDE)
@@ -243,12 +260,13 @@
                 if k == 3:
                     p3[n, c, j] = high
                     s1s[c, 1, 1, n, j] = low.astype(BF16)
-            if send is not None:
+
+        loop(body)
+        if send is not None:
+            for n in range(TILES):
                 for c in (0, 1):
                     for d in (0, 1):
                         s1_copy(c, d, send, n).start()
-
-        loop(body)
 
     def weight_tile(n, group):
         return lax.dot_general(
@@ -274,16 +292,16 @@
 
     score_chunk(chunk_a)
     query_chunk(chunk_a, None)
+    for c in (0, 1):
+        ag[c, 4, 2].wait_recv()
+        ag[c, 4, 3].wait_recv()
+        p2a(c, 2)
     for copy in meta_xy:
         copy.wait_recv()
     for d in range(SIDE * SIDE):
         if d >= SIDE and d % SIDE:
             prepare(d)
     for c in (0, 1):
-        ag[c, 4, 2].wait_recv()
-        ag[c, 4, 3].wait_recv()
-        p2a(c, 2)
-    for c in (0, 1):
         p2b(c, 0)
     score_chunk(chunk_b)
     query_chunk(chunk_b, None)
@@ -310,8 +328,8 @@
             ag[c, j, 2].wait_recv()
             ag[c, j, 3].wait_recv()
     score_chunk(chunk_f)
+    weight_chunk(chunk_e + chunk_f)
     query_chunk(chunk_f, 0)
-    weight_chunk(chunk_e + chunk_f)
 
     def z_copy(d, t, n):
         sem = (z_ss.at[d, t, n], z_rs.at[d, t, n], zdev(1 - 2 * d))
@@ -396,29 +414,37 @@
             qg_ref[c, :QUART, cols] = p0[n, c, 0, :QUART] + s2r[c, 1, n, 1].astype(F32) + s3r[c, 0, n]
             qg_ref[c, QUART:, cols] = p0[n, c, 0, QUART:] + s2r[c, 0, n, 1].astype(F32) + s3r[c, 1, n]
 
+    @pl.when(odd == 0)
+    def _():
+        pl.semaphore_wait(met, 2)
+
     for n in range(TILES):
         x_copy(n).wait_recv()
         z_hop(0, n)
+    z_hop(1, 0)
+    z_hop(1, 1)
     s1_mid(0)
+    z_hop(1, 2)
+    z_hop(1, 3)
     s1_mid(1)
-    for n in range(TILES):
-        z_hop(1, n)
     s1_mid(2)
-    s1_mid(3)
     z_hop(2, 0)
     z_hop(2, 1)
-    s1_end(0)
+    s1_mid(3)
     z_hop(2, 2)
     z_hop(2, 3)
+    s1_end(0)
     s1_end(1)
     z_hop(3, 0)
+    s1_end(2)
     z_hop(3, 1)
-    s1_end(2)
+    s1_end(3)
+    s2_mid(0)
     z_hop(3, 2)
+    s2_mid(1)
     z_hop(3, 3)
-    s1_end(3)
-    for n in range(TILES):
-        s2_mid(n)
+    s2_mid(2)
+    s2_mid(3)
     for n in range(TILES):
         s2_end(n)
     for n in range(TILES):
@@ -477,11 +503,12 @@
             pltpu.VMEM((2, TILES, 16, dim), F32),
             dma((7,)),
             dma((3, 4)), dma((3, 4)),
-            dma((2, 5, 4)), dma((2, 5, 4)),
+            dma((2, 6, 4)), dma((2, 6, 4)),
             dma((2, 2, 3, TILES)), dma((2, 2, 3, TILES)),
             dma((2, 2, 2, TILES)), dma((2, 2, 2, TILES)),
             dma((TILES,)), dma((TILES,)),
             dma((2, 4, TILES)), dma((2, 4, TILES)),
+            pltpu.SemaphoreType.REGULAR,
         ],
         compiler_params=pltpu.CompilerParams(
             collective_id=0, has_side_effects=True, vmem_limit_bytes=66_256_896

time: 63.6 us -> 62.4 us (0.981)
  Pallas kernels: 61.4 us -> 59.8 us
    pallas_call x1, Pallas kernels: 61.4 us -> 59.8 us  [per_device(): pl.pallas_call(kernel, out_shape=(pltpu.VMEM((2, HALF, dim), F32), pltpu....]
where the time goes in v4:
time: 62.4 us; the launch traced here: 61.9 us
  Pallas kernels  59.8 us (96%)
  local copies, waits for them, and re-layouts  1.5 us (2%)
  between operations  0.64 us (1%)
    pallas_call x1, Pallas kernels, per_device(): pl.pallas_call(kernel, out_shape=(pltpu.VMEM((2, HALF, dim), F32), pltpu....  59.8 us
    unnamed x2, local copies, waits for them, and re-layouts  1.5 us

profile of v4, /device:TPU:32, one launch (start us, length us, event | category | flops | bytes accessed | tf_op | source)
XLA Modules:
  0.0 61.9 jit_solution(15121456902182050572)
XLA Ops:
  0.6 59.8 %shard_map.77 = (f32[2,64,1024]{2,1,0:T(8,128)S(1)}, f32[8,8,1024]{2,1,0:T(8,128)S(1)}) custom-call(bf16[2,64,1024]{2,1,0:T(8,128)(2,1)} %bitcast.7, bf16[1024,1024]{1,0:T(8,128)(2,1)} %bitcast.6, f32[8,128]{1,0:T(8,128)} %prop_hbm.1, s32[8,128]{1,0:T(8,128)} %bitcast.8, s32[1,48]{1,0:T(1,128)} %list_hbm.1, s32[1,128]{1,0:T(1,128)} %bitcast.9), custom_call_target="tpu_custom_call" | custom-call | tf_op jit(solution)/shard_map/pallas_call | solution.py:469
  60.4 0.8 %copy.10 = f32[128,1024]{1,0:T(8,128)} copy(f32[128,1024]{1,0:T(8,128)S(1)} %bitcast.5) | data formatting | bytes 1048576
  61.2 0.7 %copy.11 = f32[8,8,1024]{2,1,0:T(8,128)} copy(f32[8,8,1024]{2,1,0:T(8,128)S(1)} %get-tuple-element.7) | data formatting | bytes 524288
